TPU v7x, 32 devices: a whole 2x2x4 slice. The times are simulated.
32 devices in a mesh: bulk: 4 (over y, x), cuts: 8 (over z, core).
Axes of the slice: x: 2, y: 2, z: 4, core: 2. Of those that a mesh axis runs over, the one named last changes fastest.
Arguments:
- amplitudes: bfloat16 [16384, 8192], P('bulk', 'cuts'), may hold values from -6 to 6
- amp_tiles: int32 [128, 64], P('bulk', 'cuts'), may hold values from 0 to 1, as said below
- occ_coupling: bfloat16 [128, 128], replicated, may hold values from -0.5 to 0.5
- integrals: bfloat16 [8192, 2048], P('cuts'), may hold values from -0.09375 to 0.09375
- int_tiles: int32 [64, 16], P('cuts'), may hold values from 0 to 1, as said below
Outputs:
- residual: bfloat16 [2048, 16384], P('cuts', 'bulk')
Inputs may be any that keep to these rules, and one draw needn't show every extreme that they name: `amp_tiles`: 1 where a tile is kept; kept tiles follow the distance, round a cycle of fragments, between the fragments of the two tile indices: each row of tiles keeps a band of columns near its own fragment and one near the fragment opposite on the cycle, whose width varies from group to group of rows. `int_tiles`: 1 where a tile is kept; kept tiles follow the distance, round a cycle of fragments, between the fragments of the two tile indices: each row of tiles keeps a band of columns near its own fragment and one near the fragment opposite on the cycle, whose width varies from group to group of rows.
All inputs are finite; a program needn't handle non-finite values.
Results may differ from a plain program's by a relative error of at most 0.0095.
Values may be sent and summed in bfloat16 or wider, within the bound.
A program may use at most 128 MiB of HBM per device.

v0:
```python
import jax
import jax.numpy as jnp
from jax import lax
from jax.sharding import PartitionSpec as P

TILE = 128


def keep_tiles(values, tiles):
    height, width = values.shape
    blocks = values.reshape(height // TILE, TILE, width // TILE, TILE)
    kept = blocks * tiles.astype(values.dtype)[:, None, :, None]
    return kept.reshape(height, width)


def dress_rows(gathered, occ_coupling):
    flat = gathered.reshape(gathered.shape[0], -1)
    mixed = jnp.dot(occ_coupling, flat, preferred_element_type=jnp.float32)
    return (flat.astype(jnp.float32) + mixed).astype(jnp.bfloat16).reshape(gathered.shape)


def shards(amplitudes, amp_tiles, occ_coupling, integrals, int_tiles):
    local_rows, local_cols = amplitudes.shape
    occ_all = occ_coupling.shape[0]
    first_dev = local_rows // occ_all
    amp_kept = keep_tiles(amplitudes, amp_tiles)
    int_kept = keep_tiles(integrals, int_tiles)
    out_rows = int_kept.shape[1] // lax.axis_size("cuts")
    arranged = amp_kept.reshape(first_dev, occ_all, local_cols)
    row_mask = (
        jnp.repeat(amp_tiles, TILE, axis=0)
        .astype(jnp.bfloat16)
        .reshape(first_dev, occ_all, local_cols // TILE)
    )
    gathered, mask_vir = (
        lax.all_to_all(arranged, "bulk", split_axis=1, concat_axis=0, tiled=True),
        lax.all_to_all(row_mask, "bulk", split_axis=1, concat_axis=0, tiled=True),
    )
    second_dev = gathered.shape[1]
    col_mask = jnp.repeat(mask_vir, TILE, axis=2)
    tau_vir = (dress_rows(gathered, occ_coupling) * col_mask).reshape(
        occ_all * second_dev, local_cols
    )
    total = lax.psum_scatter(
        lax.dot_general(
            int_kept, tau_vir, (((0,), (1,)), ((), ())), preferred_element_type=jnp.float32
        ).astype(jnp.bfloat16),
        "cuts",
        scatter_dimension=0,
        tiled=True,
    )
    rounded = total.reshape(out_rows, occ_all, second_dev)
    returned = lax.all_to_all(rounded, "bulk", split_axis=1, concat_axis=2, tiled=True)
    return returned.reshape(out_rows, local_rows)


def solution(mesh):
    in_specs = (P("bulk", "cuts"), P("bulk", "cuts"), P(), P("cuts", None), P("cuts", None))
    out_specs = P("cuts", "bulk")
    return jax.shard_map(shards, mesh=mesh, in_specs=in_specs, out_specs=out_specs, check_vma=False)
```

profile of v0, /device:TPU:0, one launch (start us, length us, event | category | flops | bytes accessed | tf_op | source)
XLA Modules:
  0.0 445.7 jit_solution(5595642323635965047)
XLA Ops:
  6.5 0.0 copy-start
  6.5 0.7 convert_element_type.19
  7.3 0.9 reshape.38
  8.2 5.2 %all-to-all-start.1 = ((bf16[4,2,4096]{2,1,0:T(2,128)(2,1)}), bf16[4,2,4096]{2,1,0:T(2,128)(2,1)S(1)}, u32[]{:S(2)}, u32[]{:S(2)}) async-start(bf16[4,2,4096]{2,1,0:T(2,128)(2,1)} %reshape.38), calls=%async_computation.1 | async-start | bytes 131072 | tf_op jit(solution)/shard_map/all_to_all | solution.py:37
  13.4 0.1 copy.52
  13.4 0.1 mul.31
  13.6 7.2 %broadcast_multiply_fusion = bf16[32,128,1024]{2,1,0:T(8,128)(2,1)} fusion(bf16[32,128,1024]{2,1,0:T(8,128)(2,1)} %bitcast.47, bf16[32,1024]{1,0:T(8,128)(2,1)S(1)} %bitcast.55), kind=kLoop, calls=%fused_computation.8 | loop fusion | flops 4194304 | bytes 16842752 | tf_op jit(solution)/shard_map/mul | solution.py:12
  20.8 11.3 %copy.53 = bf16[32,128,1024]{2,0,1:T(8,128)(2,1)} copy(bf16[32,128,1024]{2,1,0:T(8,128)(2,1)} %broadcast_multiply_fusion) | data formatting | bytes 16777216 | tf_op jit(solution)/shard_map/mul | solution.py:12
  32.1 0.0 copy-start.2
  32.1 0.0 all-to-all-done.1
  32.1 5.8 %all-to-all-start = ((bf16[32,128,1024]{2,0,1:T(8,128)(2,1)}), bf16[32,128,1024]{2,0,1:T(8,128)(2,1)}, u32[]{:S(2)}, u32[]{:S(2)}) async-start(bf16[32,128,1024]{2,0,1:T(8,128)(2,1)} %copy.53), calls=%async_computation | async-start | bytes 16777216 | tf_op jit(solution)/shard_map/all_to_all | solution.py:36
  37.9 0.2 reduce-scatter.2.cloned.1.call-start
  38.1 0.0 copy-done.2
  38.1 0.2 reshape.39
  38.3 0.2 copy.82
  38.5 1.6 copy.67
  40.2 90.1 %all-to-all-done = bf16[32,128,1024]{2,0,1:T(8,128)(2,1)} async-done(((bf16[32,128,1024]{2,0,1:T(8,128)(2,1)}), bf16[32,128,1024]{2,0,1:T(8,128)(2,1)}, u32[]{:S(2)}, u32[]{:S(2)}) %all-to-all-start) | async-done | bytes 8388640 | tf_op jit(solution)/shard_map/all_to_all | solution.py:36
  130.2 11.4 %copy.55 = bf16[4,32,32,1024]{3,2,1,0:T(8,128)(2,1)} copy(bf16[4,32,32,1024]{3,1,2,0:T(8,128)(2,1)} %bitcast.3) | data formatting | bytes 16777216 | tf_op jit(solution)/shard_map/all_to_all | solution.py:36
  141.6 12.9 %copy.70 = bf16[16,8,32,1024]{3,1,2,0:T(8,128)(2,1)} copy(bf16[16,8,32,1024]{3,2,1,0:T(8,128)(2,1)} %bitcast.45) | data formatting | bytes 16777216
  154.5 11.9 %copy.56 = bf16[128,32768]{0,1:T(8,128)(2,1)} copy(bf16[128,32768]{1,0:T(8,128)(2,1)} %bitcast.43) | data formatting | bytes 16777216 | tf_op jit(solution)/shard_map/reshape | solution.py:17
  166.4 0.0 copy-done
  166.4 11.4 %fusion.1 = bf16[128,32768]{0,1:T(8,128)(2,1)} fusion(bf16[128,32768]{1,0:T(8,128)(2,1)} %bitcast.44, bf16[128,128]{1,0:T(8,128)(2,1)S(1)} %copy-done, bf16[128,32768]{0,1:T(8,128)(2,1)} %copy.56), kind=kOutput, calls=%fused_computation.2 | convolution fusion | flops 1086324736 | bytes 25198592 | tf_op jit(solution)/shard_map/dot_general | solution.py:18
  177.8 12.0 %copy.57 = bf16[128,32768]{1,0:T(8,128)(2,1)} copy(bf16[128,32768]{0,1:T(8,128)(2,1)} %fusion.1) | data formatting | bytes 16777216 | tf_op jit(solution)/shard_map/convert_element_type | solution.py:19
  189.7 13.5 %reshape.34 = bf16[4096,1024]{1,0:T(8,128)(2,1)} reshape(bf16[128,32768]{1,0:T(8,128)(2,1)} %copy.57) | data formatting | bytes 16777216 | tf_op jit(solution)/shard_map/reshape | solution.py:19
  203.2 2.6 mul.28
  205.8 4.9 %broadcast_in_dim.9 = bf16[128,32,8,128]{3,2,1,0:T(8,128)(2,1)S(1)} broadcast(bf16[128,32,8]{2,1,0:T(8,128)(2,1)S(1)} %bitcast.51), dimensions={0,1,2} | broadcast | bytes 8454144 | tf_op jit(solution)/shard_map/broadcast_in_dim | solution.py:40
  210.7 26.5 %convolution_convert_fusion = bf16[2048,4096]{1,0:T(8,128)(2,1)} fusion(bf16[4096,1024]{1,0:T(8,128)(2,1)} %reshape.34, bf16[512,8,8,128]{3,2,1,0:T(8,128)(2,1)S(1)} %bitcast.46, bf16[1024,2048]{1,0:T(8,128)(2,1)} %param.8, bf16[128,8,16,128]{3,2,1,0:T(8,128)(2,1)} %bitcast.52), kind=kOutput, calls=%fused_computation.3 | convolution fusion | flops 17194549248 | bytes 41943040 | tf_op jit(solution)/shard_map/dot_general | solution.py:45
  237.2 0.0 reduce-scatter.2.cloned.1.call-update
  237.2 0.0 copy-start.1
  237.2 168.7 %reduce-scatter.2.cloned.1.call-done = bf16[256,4096]{1,0:T(8,128)(2,1)} async-done(((bf16[2048,4096]{1,0:T(8,128)(2,1)}), bf16[256,4096]{1,0:T(8,128)(2,1)}) %reduce-scatter.2.cloned.1.call-update) | async-done | bytes 2097168 | tf_op jit(solution)/shard_map/reduce_scatter | solution.py:44
  405.9 3.3 copy.61
  409.2 26.7 %all_to_all.48 = bf16[256,128,32]{0,2,1:T(8,128)(2,1)S(1)} all-to-all(bf16[256,128,32]{0,2,1:T(8,128)(2,1)S(1)} %bitcast.48), channel_id=1, replica_groups=mesh['bulk'=4,'cuts'=8] {'bulk'}, dimensions={1} | all-to-all | bytes 4194304 | tf_op jit(solution)/shard_map/all_to_all | solution.py:53
  435.8 0.2 copy.62
  436.0 2.9 copy.63
  438.9 0.0 copy-done.1
  (3 shorter events, 0.1 us)
Async XLA Ops:
  6.5 159.9 %copy-start = (bf16[128,128]{1,0:T(8,128)(2,1)S(1)}, bf16[128,128]{1,0:T(8,128)(2,1)}, u32[]{:S(2)}) copy-start(bf16[128,128]{1,0:T(8,128)(2,1)} %param.7) | copy-start | bytes 98308
  8.2 23.9 %all-to-all-start.1 = ((bf16[4,2,4096]{2,1,0:T(2,128)(2,1)}), bf16[4,2,4096]{2,1,0:T(2,128)(2,1)S(1)}, u32[]{:S(2)}, u32[]{:S(2)}) async-start(bf16[4,2,4096]{2,1,0:T(2,128)(2,1)} %reshape.38), calls=%async_computation.1 | async-start | bytes 131072 | tf_op jit(solution)/shard_map/all_to_all | solution.py:37
  32.1 6.0 %copy-start.2 = (s32[8,16]{1,0:T(8,128)S(1)}, s32[8,16]{1,0:T(8,128)}, u32[]{:S(2)}) copy-start(s32[8,16]{1,0:T(8,128)} %param.9) | copy-start | bytes 1540
  32.1 98.1 %all-to-all-start = ((bf16[32,128,1024]{2,0,1:T(8,128)(2,1)}), bf16[32,128,1024]{2,0,1:T(8,128)(2,1)}, u32[]{:S(2)}, u32[]{:S(2)}) async-start(bf16[32,128,1024]{2,0,1:T(8,128)(2,1)} %copy.53), calls=%async_computation | async-start | bytes 16777216 | tf_op jit(solution)/shard_map/all_to_all | solution.py:36
  37.9 368.0 %reduce-scatter.2.cloned.1.call-start = ((), (), s32[]{:S(2)}) async-start(), calls=%async_computation.4 | async-start | bytes 18874368 | tf_op jit(solution)/shard_map/reduce_scatter | solution.py:44
  237.2 201.7 %copy-start.1 = (bf16[128,128]{1,0:T(8,128)(2,1)S(1)}, bf16[128,128]{1,0:T(8,128)(2,1)}, u32[]{:S(2)}) copy-start(bf16[128,128]{1,0:T(8,128)(2,1)} %param.7) | copy-start | bytes 98308
Sparse Core Ops, SparseCore 0:
  237.3 168.5 reduce-scatter.1
where the time goes:
time: 447 us; the launch traced here: 446 us
  waiting for transfers between devices  259 us (58%)
  local copies, waits for them, and re-layouts  89.9 us (20%)
  matrix products  37.9 us (8%)
  blocking collectives  26.7 us (6%)
  between operations  13.5 us (3%)
  starting transfers between devices  11.2 us (3%)
  other arithmetic  7.89 us (2%)
    reduce_scatter x1, waiting for transfers between devices, shards(): lax.psum_scatter(lax.dot_general(int_kept, tau_vir, (((0,), (1,)), ((), (...  169 us
    all_to_all x1, waiting for transfers between devices, shards(): lax.all_to_all(arranged, 'bulk', split_axis=1, concat_axis=0, tiled=True)  90.1 us
    all_to_all x1, blocking collectives, shards(): lax.all_to_all(rounded, 'bulk', split_axis=1, concat_axis=2, tiled=True)  26.7 us
    dot_general x1, matrix products, shards(): lax.dot_general(int_kept, tau_vir, (((0,), (1,)), ((), ())), preferred_el...  26.5 us
    unnamed x11, local copies, waits for them, and re-layouts  14 us
    mul x3, local copies, waits for them, and re-layouts, keep_tiles(): kept = blocks * tiles.astype(values.dtype)[:, None, :, None]  14 us
    reshape x1, local copies, waits for them, and re-layouts, dress_rows(): (flat.astype(jnp.float32) + mixed).astype(jnp.bfloat16)  13.5 us
    convert_element_type x1, local copies, waits for them, and re-layouts, dress_rows(): (flat.astype(jnp.float32) + mixed).astype(jnp.bfloat16)  12 us
  transfers between devices with their start and end apart: 3, of which 2 were waited for; matrix products, arithmetic and copies ran while one was open for 5% of the time, Pallas kernels for 0%

commit v1 on v0

v1 whole, which is shorter than its diff:
```python
import functools

import jax
import jax.numpy as jnp
from jax import lax
from jax.experimental import pallas as pl
from jax.experimental.pallas import tpu as pltpu
from jax.sharding import PartitionSpec as P

TILE = 128
CHUNKS = 4


def keep_tiles(values, tiles):
    height, width = values.shape
    blocks = values.reshape(height // TILE, TILE, width // TILE, TILE)
    kept = blocks * tiles.astype(values.dtype)[:, None, :, None]
    return kept.reshape(height, width)


def ladder_kernel(rows_at, amp_ref, mask_ref, occ_ref, int_ref, out_ref):
    mask = mask_ref[...]
    occ = occ_ref[...]
    slabs = []
    for at in range(rows_at):
        pieces = [amp_ref[src, at] for src in range(amp_ref.shape[0])]
        slab = jnp.concatenate(pieces, axis=0) * mask
        mixed = jnp.dot(occ, slab, preferred_element_type=jnp.float32)
        dressed = (slab.astype(jnp.float32) + mixed).astype(jnp.bfloat16)
        slabs.append(dressed * mask)
    tau = jnp.concatenate(slabs, axis=0)
    width = out_ref.shape[2]
    for owner in range(out_ref.shape[0]):
        part = jnp.dot(
            tau, int_ref[:, owner * width : (owner + 1) * width], preferred_element_type=jnp.float32
        )
        out_ref[owner] = part.astype(jnp.bfloat16)


def ladder(arrived, mask, occ_coupling, int_kept, owners):
    sources, seconds, firsts, cols = arrived.shape
    occ_all = occ_coupling.shape[0]
    width = int_kept.shape[1] // owners
    rows_at = 2 if seconds % 2 == 0 else 1
    block = rows_at * occ_all
    rows = seconds * occ_all
    flops = 2 * rows * cols * (occ_all + owners * width)
    moved = 2 * (rows * cols + cols * owners * width + rows * owners * width)
    return pl.pallas_call(
        functools.partial(ladder_kernel, rows_at),
        grid=(seconds // rows_at,),
        in_specs=[
            pl.BlockSpec((sources, rows_at, firsts, cols), lambda g: (0, g, 0, 0)),
            pl.BlockSpec((occ_all, cols), lambda g: (0, 0)),
            pl.BlockSpec((occ_all, occ_all), lambda g: (0, 0)),
            pl.BlockSpec((cols, owners * width), lambda g: (0, 0)),
        ],
        out_specs=pl.BlockSpec((owners, block, width), lambda g: (0, g, 0)),
        out_shape=jax.ShapeDtypeStruct((owners, rows, width), jnp.bfloat16),
        compiler_params=pltpu.CompilerParams(vmem_limit_bytes=40 * 1024 * 1024),
        cost_estimate=pl.CostEstimate(flops=flops, bytes_accessed=moved, transcendentals=0),
        name="ladder",
    )(arrived, mask, occ_coupling, int_kept)


def shards(amplitudes, amp_tiles, occ_coupling, integrals, int_tiles):
    local_rows, local_cols = amplitudes.shape
    occ_all = occ_coupling.shape[0]
    first_dev = local_rows // occ_all
    peers = lax.axis_size("bulk")
    owners = lax.axis_size("cuts")
    second_dev = occ_all // peers
    step = second_dev // CHUNKS
    tiles_all = lax.all_gather(amp_tiles.astype(jnp.bfloat16), "bulk", axis=0, tiled=True)
    mask = jnp.repeat(tiles_all, TILE, axis=1)
    int_kept = keep_tiles(integrals, int_tiles)
    by_owner = amplitudes.reshape(first_dev, peers, CHUNKS, step, local_cols)
    finished = []
    for at in range(CHUNKS):
        sent = by_owner[:, :, at].transpose(1, 2, 0, 3)
        arrived = lax.all_to_all(sent, "bulk", split_axis=0, concat_axis=0, tiled=True)
        partial = ladder(arrived, mask, occ_coupling, int_kept, owners)
        total = lax.psum_scatter(partial, "cuts", scatter_dimension=0, tiled=False)
        width = total.shape[1]
        back = total.reshape(step, peers, first_dev, width)
        back = lax.all_to_all(back, "bulk", split_axis=1, concat_axis=1, tiled=True)
        finished.append(back)
    joined = jnp.stack(finished, axis=0)
    out = joined.transpose(4, 3, 2, 0, 1)
    return out.reshape(out.shape[0], local_rows)


def solution(mesh):
    in_specs = (P("bulk", "cuts"), P("bulk", "cuts"), P(), P("cuts", None), P("cuts", None))
    out_specs = P("cuts", "bulk")
    return jax.shard_map(shards, mesh=mesh, in_specs=in_specs, out_specs=out_specs, check_vma=False)
```

time: 447 us -> 290 us (0.65)
  waiting for transfers between devices: 259 us -> 82.7 us
  blocking collectives: 26.7 us -> 103 us
  local copies, waits for them, and re-layouts: 89.9 us -> 41.5 us
  matrix products: 37.9 us -> 0 us
  Pallas kernels: 0 us -> 24.3 us
  starting transfers between devices: 11.2 us -> 19.6 us
    reduce_scatter x1 -> x4, waiting for transfers between devices: 169 us -> 72.4 us  [shards(): total = lax.psum_scatter(partial, 'cuts', scatter_dimension=0, tiled=False)]
    all_to_all x2 -> x5, waiting for transfers between devices: 90.1 us -> 10.3 us  [the longest x4 10.3 us: shards(): back = lax.all_to_all(back, 'bulk', split_axis=1, concat_axis=1, tiled=True)]
    all_to_all x1 -> x3, blocking collectives: 26.7 us -> 75.2 us  [shards(): lax.all_to_all(sent, 'bulk', split_axis=0, concat_axis=0, tiled=True)]
    dot_general x2 -> x0, matrix products: 37.9 us -> none  [the longest x1 26.5 us: shards(): lax.dot_general(int_kept, tau_vir, (((0,), (1,)), ((), ())), preferred_el...]
    all_gather x0 -> x1, blocking collectives: none -> 28 us  [shards(): lax.all_gather(amp_tiles.astype(jnp.bfloat16), 'bulk', axis=0, tiled=True)]
    reshape x3 -> x1, local copies, waits for them, and re-layouts: 28.2 us -> 2.86 us  [shards(): return out.reshape(out.shape[0], local_rows)]
    pallas_call x0 -> x4, Pallas kernels: none -> 24.3 us  [ladder(): pl.pallas_call(functools.partial(ladder_kernel, rows_at), grid=(seconds /...]
    mul x3 -> x1, local copies, waits for them, and re-layouts: 14 us -> 0.61 us  [keep_tiles(): kept = blocks * tiles.astype(values.dtype)[:, None, :, None]]
  transfers between devices with their start and end apart: 3 -> 9, of which waited for: 2 -> 4; matrix products, arithmetic and copies ran while one was open for 5% -> 6% of each run, Pallas kernels for 0% -> 6%
where the time goes in v1:
time: 290 us; the launch traced here: 289 us
  blocking collectives  103 us (36%)
  waiting for transfers between devices  82.7 us (29%)
  local copies, waits for them, and re-layouts  41.5 us (14%)
  Pallas kernels  24.3 us (8%)
  starting transfers between devices  19.6 us (7%)
  between operations  13.3 us (5%)
  other arithmetic  4.2 us (1%)
    all_to_all x3, blocking collectives, shards(): lax.all_to_all(sent, 'bulk', split_axis=0, concat_axis=0, tiled=True)  75.2 us
    reduce_scatter x4, waiting for transfers between devices, shards(): total = lax.psum_scatter(partial, 'cuts', scatter_dimension=0, tiled=False)  72.4 us
    all_gather x1, blocking collectives, shards(): lax.all_gather(amp_tiles.astype(jnp.bfloat16), 'bulk', axis=0, tiled=True)  28 us
    pallas_call x4, Pallas kernels, ladder(): pl.pallas_call(functools.partial(ladder_kernel, rows_at), grid=(seconds /...  24.3 us
    unnamed x36, local copies, waits for them, and re-layouts  22.4 us
    all_to_all x4, starting transfers between devices, shards(): back = lax.all_to_all(back, 'bulk', split_axis=1, concat_axis=1, tiled=True)  14.2 us
    all_to_all x4, waiting for transfers between devices, shards(): back = lax.all_to_all(back, 'bulk', split_axis=1, concat_axis=1, tiled=True)  10.3 us
    another operation x4, local copies, waits for them, and re-layouts, shards(): back = total.reshape(step, peers, first_dev, width)  8.56 us
  transfers between devices with their start and end apart: 9, of which 4 were waited for; matrix products, arithmetic and copies ran while one was open for 6% of the time, Pallas kernels for 6%

profile of v1, /device:TPU:0, one launch (start us, length us, event | category | flops | bytes accessed | tf_op | source)
XLA Modules:
  0.0 289.0 jit_solution(9471586911341265458)
XLA Ops:
  6.5 5.9 %fusion = (bf16[32,4,1,8,1024]{4,3,2,1,0:T(8,128)(2,1)S(1)}, bf16[32,4,1,8,1024]{4,3,2,1,0:T(8,128)(2,1)}, bf16[32,4,1,8,1024]{4,3,2,1,0:T(8,128)(2,1)}, bf16[32,4,1,8,1024]{4,3,2,1,0:T(8,128)(2,1)}) fusion(bf16[32,4,4,8,1024]{4,3,2,1,0:T(8,128)(2,1)} %bitcast.56), kind=kLoop, calls=%fused_computation.12 | loop fusion | bytes 16777216 | tf_op jit(solution)/shard_map/slice | solution.py:80
  12.4 2.6 copy.54
  15.0 5.3 %all-to-all-start = ((bf16[4,8,32,1024]{3,2,1,0:T(8,128)(2,1)}), bf16[4,8,32,1024]{3,2,1,0:T(8,128)(2,1)S(1)}, u32[]{:S(2)}, u32[]{:S(2)}) async-start(bf16[4,8,32,1024]{3,2,1,0:T(8,128)(2,1)} %bitcast.57), calls=%async_computation | async-start | bytes 4194304 | tf_op jit(solution)/shard_map/all_to_all | solution.py:81
  20.3 28.0 %all-gather = bf16[4,32,8]{1,2,0:T(8,128)(2,1)S(1)} all-gather(bf16[1,32,8]{1,2,0:T(8,128)(2,1)S(1)} %convert_bitcast_fusion), channel_id=1, replica_groups=mesh['bulk'=4,'cuts'=8] {'bulk'}, dimensions={0}, use_global_device_ids=true | all-gather | bytes 2560 | tf_op jit(solution)/shard_map/all_gather | solution.py:74
  48.3 0.1 copy.33
  48.4 0.2 broadcast_in_dim.4
  48.6 0.6 mul.11
  49.2 1.6 copy-done.12
  50.8 2.9 %bitcast_multiply_fusion.int_ref = bf16[1024,2048]{1,0:T(8,128)(2,1)} fusion(bf16[1024,2048]{1,0:T(8,128)(2,1)S(1)} %copy-done.12, bf16[128,8,16,128]{3,2,1,0:T(8,128)(2,1)S(1)} %bitcast.55), kind=kLoop, calls=%fused_computation | loop fusion | flops 2097152 | bytes 12582912 | tf_op jit(solution)/shard_map/mul | solution.py:17
  53.7 2.2 copy-done
  55.9 6.1 %ladder.4 = bf16[8,1024,256]{2,1,0:T(8,128)(2,1)S(1)} custom-call(bf16[4,8,32,1024]{3,2,1,0:T(8,128)(2,1)S(1)} %all-to-all-done.amp_ref, bf16[128,1024]{1,0:T(8,128)(2,1)S(1)} %bitcast.51, bf16[128,128]{1,0:T(8,128)(2,1)S(1)} %copy-done.8, bf16[1024,2048]{1,0:T(8,128)(2,1)S(1)} %copy-done), custom_call_target="tpu_custom_call" | custom-call | flops 4563402752 | bytes 10485760 | tf_op jit(solution)/shard_map/ladder/pallas_call | solution.py:49
  62.0 1.9 copy-done.4
  64.0 0.0 reduce-scatter.9.cloned.1.call-start
  64.0 1.5 copy-done.11
  65.5 1.2 copy.52
  66.7 26.3 %all_to_all.40.amp_ref = bf16[4,8,32,1024]{3,2,1,0:T(8,128)(2,1)S(1)} all-to-all(bf16[4,8,32,1024]{3,2,1,0:T(8,128)(2,1)S(1)} %bitcast.59), channel_id=1, replica_groups=mesh['bulk'=4,'cuts'=8] {'bulk'}, dimensions={0} | all-to-all | bytes 4194304 | tf_op jit(solution)/shard_map/all_to_all | solution.py:81
  93.0 6.1 %ladder.6 = bf16[8,1024,256]{2,1,0:T(8,128)(2,1)S(1)} custom-call(bf16[4,8,32,1024]{3,2,1,0:T(8,128)(2,1)S(1)} %all_to_all.40.amp_ref, bf16[128,1024]{1,0:T(8,128)(2,1)S(1)} %bitcast.52, bf16[128,128]{1,0:T(8,128)(2,1)S(1)} %copy-done.8, bf16[1024,2048]{1,0:T(8,128)(2,1)S(1)} %copy-done.1), custom_call_target="tpu_custom_call" | custom-call | flops 4563402752 | bytes 10485760 | tf_op jit(solution)/shard_map/ladder/pallas_call | solution.py:49
  99.1 1.9 copy-done.5
  101.1 0.0 reduce-scatter.7.cloned.1.call-start
  101.1 1.6 copy-done.10
  102.7 1.2 copy.53
  103.8 25.1 %all_to_all.41.amp_ref = bf16[4,8,32,1024]{3,2,1,0:T(8,128)(2,1)S(1)} all-to-all(bf16[4,8,32,1024]{3,2,1,0:T(8,128)(2,1)S(1)} %bitcast.60), channel_id=1, replica_groups=mesh['bulk'=4,'cuts'=8] {'bulk'}, dimensions={0} | all-to-all | bytes 4194304 | tf_op jit(solution)/shard_map/all_to_all | solution.py:81
  128.9 6.1 %ladder.5 = bf16[8,1024,256]{2,1,0:T(8,128)(2,1)S(1)} custom-call(bf16[4,8,32,1024]{3,2,1,0:T(8,128)(2,1)S(1)} %all_to_all.41.amp_ref, bf16[128,1024]{1,0:T(8,128)(2,1)S(1)} %bitcast.53, bf16[128,128]{1,0:T(8,128)(2,1)S(1)} %copy-done.8, bf16[1024,2048]{1,0:T(8,128)(2,1)S(1)} %copy-done.2), custom_call_target="tpu_custom_call" | custom-call | flops 4563402752 | bytes 10485760 | tf_op jit(solution)/shard_map/ladder/pallas_call | solution.py:49
  135.0 2.0 copy-done.6
  137.0 0.0 reduce-scatter.11.cloned.1.call-start
  137.1 1.5 copy-done.9
  138.6 1.2 copy.51
  139.8 23.8 %all_to_all.42.amp_ref = bf16[4,8,32,1024]{3,2,1,0:T(8,128)(2,1)S(1)} all-to-all(bf16[4,8,32,1024]{3,2,1,0:T(8,128)(2,1)S(1)} %bitcast.61), channel_id=1, replica_groups=mesh['bulk'=4,'cuts'=8] {'bulk'}, dimensions={0} | all-to-all | bytes 4194304 | tf_op jit(solution)/shard_map/all_to_all | solution.py:81
  163.6 6.1 %ladder.7 = bf16[8,1024,256]{2,1,0:T(8,128)(2,1)S(1)} custom-call(bf16[4,8,32,1024]{3,2,1,0:T(8,128)(2,1)S(1)} %all_to_all.42.amp_ref, bf16[128,1024]{1,0:T(8,128)(2,1)S(1)} %bitcast.54, bf16[128,128]{1,0:T(8,128)(2,1)S(1)} %copy-done.8, bf16[1024,2048]{1,0:T(8,128)(2,1)S(1)} %copy-done.3), custom_call_target="tpu_custom_call" | custom-call | flops 4563402752 | bytes 10485760 | tf_op jit(solution)/shard_map/ladder/pallas_call | solution.py:49
  169.7 2.0 copy-done.7
  171.7 2.2 copy.21
  173.9 3.5 %all-to-all-start.1 = ((bf16[8,4,32,256]{3,0,2,1:T(8,128)(2,1)}), bf16[8,4,32,256]{3,0,2,1:T(8,128)(2,1)S(1)}, u32[]{:S(2)}, u32[]{:S(2)}) async-start(bf16[8,4,32,256]{3,0,2,1:T(8,128)(2,1)} %copy.21), calls=%async_computation.2 | async-start | bytes 1048576 | tf_op jit(solution)/shard_map/all_to_all | solution.py:86
  177.4 2.1 copy.27
  179.5 4.7 %all-to-all-done.1 = bf16[8,4,32,256]{3,0,2,1:T(8,128)(2,1)S(1)} async-done(((bf16[8,4,32,256]{3,0,2,1:T(8,128)(2,1)}), bf16[8,4,32,256]{3,0,2,1:T(8,128)(2,1)S(1)}, u32[]{:S(2)}, u32[]{:S(2)}) %all-to-all-start.1) | async-done | bytes 524320 | tf_op jit(solution)/shard_map/all_to_all | solution.py:86
  184.2 3.5 %all-to-all-start.5 = ((bf16[8,4,32,256]{3,0,2,1:T(8,128)(2,1)}), bf16[8,4,32,256]{3,0,2,1:T(8,128)(2,1)S(1)}, u32[]{:S(2)}, u32[]{:S(2)}) async-start(bf16[8,4,32,256]{3,0,2,1:T(8,128)(2,1)} %copy.27), calls=%async_computation.8 | async-start | bytes 1048576 | tf_op jit(solution)/shard_map/all_to_all | solution.py:86
  187.7 27.8 %reduce-scatter.7.cloned.1.call-done = bf16[1,1024,256]{2,1,0:T(8,128)(2,1)} async-done(((bf16[8,1024,256]{2,1,0:T(8,128)(2,1)}), bf16[1,1024,256]{2,1,0:T(8,128)(2,1)}) %reduce-scatter.7.cloned.1.call-update) | async-done | bytes 524304 | tf_op jit(solution)/shard_map/reduce_scatter | solution.py:83
  215.5 2.1 copy.24
  217.7 3.7 %all-to-all-start.3 = ((bf16[8,4,32,256]{3,0,2,1:T(8,128)(2,1)}), bf16[8,4,32,256]{3,0,2,1:T(8,128)(2,1)S(1)}, u32[]{:S(2)}, u32[]{:S(2)}) async-start(bf16[8,4,32,256]{3,0,2,1:T(8,128)(2,1)} %copy.24), calls=%async_computation.5 | async-start | bytes 1048576 | tf_op jit(solution)/shard_map/all_to_all | solution.py:86
  221.3 44.6 %reduce-scatter.11.cloned.1.call-done = bf16[1,1024,256]{2,1,0:T(8,128)(2,1)} async-done(((bf16[8,1024,256]{2,1,0:T(8,128)(2,1)}), bf16[1,1024,256]{2,1,0:T(8,128)(2,1)}) %reduce-scatter.11.cloned.1.call-update) | async-done | bytes 524304 | tf_op jit(solution)/shard_map/reduce_scatter | solution.py:83
  265.9 2.1 copy.30
  268.0 3.6 %all-to-all-start.7 = ((bf16[8,4,32,256]{3,0,2,1:T(8,128)(2,1)}), bf16[8,4,32,256]{3,0,2,1:T(8,128)(2,1)S(1)}, u32[]{:S(2)}, u32[]{:S(2)}) async-start(bf16[8,4,32,256]{3,0,2,1:T(8,128)(2,1)} %copy.30), calls=%async_computation.11 | async-start | bytes 1048576 | tf_op jit(solution)/shard_map/all_to_all | solution.py:86
  271.6 0.1 copy.58
  271.7 0.1 copy.56
  271.7 0.9 copy.57
  272.6 5.6 %all-to-all-done.7 = bf16[8,4,32,256]{3,0,2,1:T(8,128)(2,1)S(1)} async-done(((bf16[8,4,32,256]{3,0,2,1:T(8,128)(2,1)}), bf16[8,4,32,256]{3,0,2,1:T(8,128)(2,1)S(1)}, u32[]{:S(2)}, u32[]{:S(2)}) %all-to-all-start.7) | async-done | bytes 524320 | tf_op jit(solution)/shard_map/all_to_all | solution.py:86
  278.2 0.1 copy.55
  278.3 1.3 pad_maximum_fusion
  279.6 2.9 copy.32
  (34 shorter events, 0.2 us)
Async XLA Ops:
  14.9 5.3 %copy-start.13 = (s32[8,16]{1,0:T(8,128)S(1)}, s32[8,16]{1,0:T(8,128)}, u32[]{:S(2)}) copy-start(s32[8,16]{1,0:T(8,128)} %param.9) | copy-start | bytes 1540
  14.9 5.3 %copy-start.14 = (s32[32,8]{0,1:T(8,128)S(1)}, s32[32,8]{0,1:T(8,128)}, u32[]{:S(2)}) copy-start(s32[32,8]{0,1:T(8,128)} %param.6) | copy-start | bytes 3076
  15.0 38.8 %all-to-all-start = ((bf16[4,8,32,1024]{3,2,1,0:T(8,128)(2,1)}), bf16[4,8,32,1024]{3,2,1,0:T(8,128)(2,1)S(1)}, u32[]{:S(2)}, u32[]{:S(2)}) async-start(bf16[4,8,32,1024]{3,2,1,0:T(8,128)(2,1)} %bitcast.57), calls=%async_computation | async-start | bytes 4194304 | tf_op jit(solution)/shard_map/all_to_all | solution.py:81
  20.2 151.5 %reduce-scatter.5.cloned.1.call-start = ((), (), s32[]{:S(2)}) async-start(), calls=%async_computation.12 | async-start | bytes 4718592 | tf_op jit(solution)/shard_map/reduce_scatter | solution.py:83
  48.6 2.2 copy-start.12
  50.8 2.9 %copy-start.8 = (bf16[128,128]{1,0:T(8,128)(2,1)S(1)}, bf16[128,128]{1,0:T(8,128)(2,1)}, u32[]{:S(2)}) copy-start(bf16[128,128]{1,0:T(8,128)(2,1)} %occ_ref.7) | copy-start | bytes 98308
  53.7 2.2 copy-start
  62.0 1.9 copy-start.4
  63.9 1.6 copy-start.11
  64.0 113.4 %reduce-scatter.9.cloned.1.call-start = ((), (), s32[]{:S(2)}) async-start(), calls=%async_computation.14 | async-start | bytes 4718592 | tf_op jit(solution)/shard_map/reduce_scatter | solution.py:83
  66.7 26.3 %copy-start.1 = (bf16[1024,2048]{1,0:T(8,128)(2,1)S(1)}, bf16[1024,2048]{1,0:T(8,128)(2,1)}, u32[]{:S(2)}) copy-start(bf16[1024,2048]{1,0:T(8,128)(2,1)} %bitcast_multiply_fusion.int_ref) | copy-start | bytes 12582916
  99.1 1.9 copy-start.5
  101.0 1.6 copy-start.10
  101.1 114.5 %reduce-scatter.7.cloned.1.call-start = ((), (), s32[]{:S(2)}) async-start(), calls=%async_computation.13 | async-start | bytes 4718592 | tf_op jit(solution)/shard_map/reduce_scatter | solution.py:83
  103.8 25.1 %copy-start.2 = (bf16[1024,2048]{1,0:T(8,128)(2,1)S(1)}, bf16[1024,2048]{1,0:T(8,128)(2,1)}, u32[]{:S(2)}) copy-start(bf16[1024,2048]{1,0:T(8,128)(2,1)} %bitcast_multiply_fusion.int_ref) | copy-start | bytes 12582916
  135.0 2.0 copy-start.6
  137.0 1.6 copy-start.9
  137.0 128.8 %reduce-scatter.11.cloned.1.call-start = ((), (), s32[]{:S(2)}) async-start(), calls=%async_computation.15 | async-start | bytes 4718592 | tf_op jit(solution)/shard_map/reduce_scatter | solution.py:83
  139.8 23.8 %copy-start.3 = (bf16[1024,2048]{1,0:T(8,128)(2,1)S(1)}, bf16[1024,2048]{1,0:T(8,128)(2,1)}, u32[]{:S(2)}) copy-start(bf16[1024,2048]{1,0:T(8,128)(2,1)} %bitcast_multiply_fusion.int_ref) | copy-start | bytes 12582916
  169.7 2.0 copy-start.7
  173.9 10.3 %all-to-all-start.1 = ((bf16[8,4,32,256]{3,0,2,1:T(8,128)(2,1)}), bf16[8,4,32,256]{3,0,2,1:T(8,128)(2,1)S(1)}, u32[]{:S(2)}, u32[]{:S(2)}) async-start(bf16[8,4,32,256]{3,0,2,1:T(8,128)(2,1)} %copy.21), calls=%async_computation.2 | async-start | bytes 1048576 | tf_op jit(solution)/shard_map/all_to_all | solution.py:86
  184.2 33.5 %all-to-all-start.5 = ((bf16[8,4,32,256]{3,0,2,1:T(8,128)(2,1)}), bf16[8,4,32,256]{3,0,2,1:T(8,128)(2,1)S(1)}, u32[]{:S(2)}, u32[]{:S(2)}) async-start(bf16[8,4,32,256]{3,0,2,1:T(8,128)(2,1)} %copy.27), calls=%async_computation.8 | async-start | bytes 1048576 | tf_op jit(solution)/shard_map/all_to_all | solution.py:86
  217.7 50.3 %all-to-all-start.3 = ((bf16[8,4,32,256]{3,0,2,1:T(8,128)(2,1)}), bf16[8,4,32,256]{3,0,2,1:T(8,128)(2,1)S(1)}, u32[]{:S(2)}, u32[]{:S(2)}) async-start(bf16[8,4,32,256]{3,0,2,1:T(8,128)(2,1)} %copy.24), calls=%async_computation.5 | async-start | bytes 1048576 | tf_op jit(solution)/shard_map/all_to_all | solution.py:86
  268.0 10.2 %all-to-all-start.7 = ((bf16[8,4,32,256]{3,0,2,1:T(8,128)(2,1)}), bf16[8,4,32,256]{3,0,2,1:T(8,128)(2,1)S(1)}, u32[]{:S(2)}, u32[]{:S(2)}) async-start(bf16[8,4,32,256]{3,0,2,1:T(8,128)(2,1)} %copy.30), calls=%async_computation.11 | async-start | bytes 1048576 | tf_op jit(solution)/shard_map/all_to_all | solution.py:86
Sparse Core Ops, SparseCore 0:
  64.1 50.3 reduce-scatter.4
  116.8 48.1 reduce-scatter.8
  167.3 48.1 reduce-scatter.6
  217.7 48.1 reduce-scatter.10

commit v2 on v1

v2 whole, which is shorter than its diff:
```python
import functools

import jax
import jax.numpy as jnp
from jax import lax
from jax.experimental import pallas as pl
from jax.experimental.pallas import tpu as pltpu
from jax.sharding import Mesh, PartitionSpec as P

TILE = 128
CORES = 2
GROUP = ("bulk", "core")


def keep_tiles(values, tiles):
    height, width = values.shape
    blocks = values.reshape(height // TILE, TILE, width // TILE, TILE)
    kept = blocks * tiles.astype(values.dtype)[:, None, :, None]
    return kept.reshape(height, width)


def ladder_kernel(rows_at, amp_ref, mask_ref, occ_ref, int_ref, out_ref):
    occ = occ_ref[...]
    peers, cores, _, firsts, cols = amp_ref.shape
    occ_all = occ.shape[0]
    slabs = []
    for at in range(rows_at):
        halves = []
        for core in range(cores):
            mask = mask_ref[:, core * cols : (core + 1) * cols]
            pieces = [amp_ref[src, core, at] for src in range(peers)]
            slab = jnp.concatenate(pieces, axis=0) * mask
            mixed = jnp.dot(occ, slab, preferred_element_type=jnp.float32)
            dressed = (slab.astype(jnp.float32) + mixed).astype(jnp.bfloat16)
            halves.append(dressed * mask)
        slabs.append(jnp.concatenate(halves, axis=1))
    tau = jnp.concatenate(slabs, axis=0)
    width = out_ref.shape[-1]
    for owner in range(out_ref.shape[0]):
        for core in range(cores):
            start = (owner * cores + core) * width
            part = jnp.dot(
                tau, int_ref[:, start : start + width], preferred_element_type=jnp.float32
            ).astype(jnp.bfloat16)
            for at in range(rows_at):
                for peer in range(peers):
                    row = at * occ_all + peer * firsts
                    out_ref[owner, peer, core, at] = part[row : row + firsts]


def ladder(arrived, mask, occ_coupling, int_kept, owners):
    peers, cores, seconds, firsts, cols = arrived.shape
    occ_all = occ_coupling.shape[0]
    depth, total = int_kept.shape
    width = total // (owners * cores)
    rows_at = 2 if seconds % 2 == 0 else 1
    rows = seconds * occ_all
    flops = 2 * rows * depth * (occ_all + total)
    moved = 2 * (rows * depth + depth * total + rows * total)
    return pl.pallas_call(
        functools.partial(ladder_kernel, rows_at),
        grid=(seconds // rows_at,),
        in_specs=[
            pl.BlockSpec((peers, cores, rows_at, firsts, cols), lambda g: (0, 0, g, 0, 0)),
            pl.BlockSpec((occ_all, depth), lambda g: (0, 0)),
            pl.BlockSpec((occ_all, occ_all), lambda g: (0, 0)),
            pl.BlockSpec((depth, total), lambda g: (0, 0), pipeline_mode=pl.Buffered(1)),
        ],
        out_specs=pl.BlockSpec(
            (owners, peers, cores, rows_at, firsts, width), lambda g: (0, 0, 0, g, 0, 0)
        ),
        out_shape=jax.ShapeDtypeStruct(
            (owners, peers, cores, seconds, firsts, width), jnp.bfloat16
        ),
        compiler_params=pltpu.CompilerParams(vmem_limit_bytes=48 * 1024 * 1024),
        cost_estimate=pl.CostEstimate(flops=flops, bytes_accessed=moved, transcendentals=0),
        name="ladder",
    )(arrived, mask, occ_coupling, int_kept)


def chunk_sizes(seconds):
    if seconds % 16 == 0:
        unit = seconds // 16
        return [2 * unit, 4 * unit, 4 * unit, 6 * unit]
    pieces = min(4, seconds)
    return [seconds // pieces] * (pieces - 1) + [seconds - seconds // pieces * (pieces - 1)]


def shards(amplitudes, amp_tiles, occ_coupling, integrals, int_tiles):
    local_rows, local_cols = amplitudes.shape
    occ_all = occ_coupling.shape[0]
    first_dev = local_rows // occ_all
    peers = lax.axis_size("bulk")
    cores = lax.axis_size("core")
    owners = lax.axis_size("z")
    second_dev = occ_all // (peers * cores)
    int_kept = lax.all_gather(keep_tiles(integrals, int_tiles), "core", axis=0, tiled=True)
    tiles_all = lax.all_gather(amp_tiles.astype(jnp.bfloat16), GROUP, axis=0, tiled=True)
    tiles_all = tiles_all.reshape(peers, cores, first_dev, local_cols // TILE)
    tiles_all = tiles_all.transpose(0, 2, 1, 3).reshape(occ_all, cores * (local_cols // TILE))
    mask = jnp.repeat(tiles_all, TILE, axis=1)
    by_owner = amplitudes.reshape(first_dev, peers * cores, second_dev, local_cols)
    finished = []
    begin = 0
    for step in chunk_sizes(second_dev):
        sent = by_owner[:, :, begin : begin + step].transpose(1, 2, 0, 3)
        begin += step
        arrived = lax.all_to_all(sent, GROUP, split_axis=0, concat_axis=0, tiled=True)
        arrived = arrived.reshape(peers, cores, step, first_dev, local_cols)
        partial = ladder(arrived, mask, occ_coupling, int_kept, owners)
        total = lax.psum_scatter(partial, "z", scatter_dimension=0, tiled=False)
        width = total.shape[-1]
        total = total.reshape(peers * cores, step, first_dev, width)
        back = lax.all_to_all(total, GROUP, split_axis=0, concat_axis=0, tiled=True)
        finished.append(back)
    joined = jnp.concatenate(finished, axis=1).reshape(occ_all, first_dev, width)
    return joined.transpose(2, 1, 0).reshape(width, local_rows)


def solution(mesh):
    bulk, cuts = mesh.devices.shape
    split = Mesh(mesh.devices.reshape(bulk, cuts // CORES, CORES), ("bulk", "z", "core"))
    along = ("z", "core")
    in_specs = (P("bulk", along), P("bulk", along), P(), P(along, None), P(along, None))
    out_specs = P(along, "bulk")
    return jax.shard_map(shards, mesh=split, in_specs=in_specs, out_specs=out_specs, check_vma=False)
```

time: 290 us -> 285 us (0.983)
  waiting for transfers between devices: 82.7 us -> 51.4 us
  blocking collectives: 103 us -> 128 us
  Pallas kernels: 24.3 us -> 38.9 us
  starting transfers between devices: 19.6 us -> 12.7 us
  local copies, waits for them, and re-layouts: 41.5 us -> 35.9 us
    reduce_scatter x4, waiting for transfers between devices: 72.4 us -> 23.2 us  [shards(): total = lax.psum_scatter(partial, 'z', scatter_dimension=0, tiled=False)]
    all_to_all x3 -> x5, blocking collectives: 75.2 us -> 110 us  [the longest x2 70.2 us: shards(): lax.all_to_all(sent, GROUP, split_axis=0, concat_axis=0, tiled=True)]
    all_to_all x5 -> x3, waiting for transfers between devices: 10.3 us -> 28.1 us  [the longest x2 18.4 us: shards(): lax.all_to_all(sent, GROUP, split_axis=0, concat_axis=0, tiled=True)]
    pallas_call x4, Pallas kernels: 24.3 us -> 38.9 us  [ladder(): pl.pallas_call(functools.partial(ladder_kernel, rows_at), grid=(seconds /...]
    all_gather x1, blocking collectives: 28 us -> 18.5 us  [shards(): lax.all_gather(amp_tiles.astype(jnp.bfloat16), GROUP, axis=0, tiled=True)]
    another operation x4 -> x0, local copies, waits for them, and re-layouts: 8.56 us -> none  [shards(): back = total.reshape(step, peers, first_dev, width)]
    slice x1 -> x3, local copies, waits for them, and re-layouts: 5.86 us -> 13.8 us  [shards(): sent = by_owner[:, :, begin:begin + step].transpose(1, 2, 0, 3)]
    all_to_all x5 -> x3, starting transfers between devices: 19.5 us -> 12.4 us  [the longest x2 8.91 us: shards(): lax.all_to_all(sent, GROUP, split_axis=0, concat_axis=0, tiled=True)]
  transfers between devices with their start and end apart: 9 -> 8, of which waited for: 4 -> 3; matrix products, arithmetic and copies ran while one was open for 6% -> 8% of each run, Pallas kernels for 6% -> 14%
where the time goes in v2:
time: 285 us; the launch traced here: 284 us
  blocking collectives  128 us (45%)
  waiting for transfers between devices  51.4 us (18%)
  Pallas kernels  38.9 us (14%)
  local copies, waits for them, and re-layouts  35.9 us (13%)
  between operations  13.3 us (5%)
  starting transfers between devices  12.7 us (4%)
  other arithmetic  3.82 us (1%)
    all_to_all x2, blocking collectives, shards(): lax.all_to_all(sent, GROUP, split_axis=0, concat_axis=0, tiled=True)  70.2 us
    all_to_all x3, blocking collectives, shards(): back = lax.all_to_all(total, GROUP, split_axis=0, concat_axis=0, tiled=True)  39.6 us
    pallas_call x4, Pallas kernels, ladder(): pl.pallas_call(functools.partial(ladder_kernel, rows_at), grid=(seconds /...  38.9 us
    reduce_scatter x4, waiting for transfers between devices, shards(): total = lax.psum_scatter(partial, 'z', scatter_dimension=0, tiled=False)  23.2 us
    all_gather x1, blocking collectives, shards(): lax.all_gather(amp_tiles.astype(jnp.bfloat16), GROUP, axis=0, tiled=True)  18.5 us
    all_to_all x2, waiting for transfers between devices, shards(): lax.all_to_all(sent, GROUP, split_axis=0, concat_axis=0, tiled=True)  18.4 us
    unnamed x20, local copies, waits for them, and re-layouts  16.9 us
    slice x3, local copies, waits for them, and re-layouts, shards(): sent = by_owner[:, :, begin:begin + step].transpose(1, 2, 0, 3)  13.8 us
  transfers between devices with their start and end apart: 8, of which 3 were waited for; matrix products, arithmetic and copies ran while one was open for 8% of the time, Pallas kernels for 14%

profile of v2, /device:TPU:0, one launch (start us, length us, event | category | flops | bytes accessed | tf_op | source)
XLA Modules:
  0.0 284.3 jit_solution(2805409128624653419)
XLA Ops:
  6.5 0.7 convert_element_type.7
  7.2 0.6 mul.11
  7.8 1.6 copy-done.5
  9.4 2.9 %bitcast_multiply_fusion = bf16[1024,2048]{1,0:T(8,128)(2,1)} fusion(bf16[1024,2048]{1,0:T(8,128)(2,1)S(1)} %copy-done.5, bf16[128,8,16,128]{3,2,1,0:T(8,128)(2,1)S(1)} %bitcast.50), kind=kLoop, calls=%fused_computation | loop fusion | flops 2097152 | bytes 12582912 | tf_op jit(solution)/shard_map/mul | solution.py:18
  12.3 0.0 all-gather.3.cloned.1.call-update
  12.3 3.3 %slice.16 = bf16[32,8,2,1024]{3,2,1,0:T(2,128)(2,1)S(1)} slice(bf16[32,8,16,1024]{3,2,1,0:T(8,128)(2,1)} %bitcast.52), slice={[0:32], [0:8], [0:2], [0:1024]} | slice | bytes 2097152 | tf_op jit(solution)/shard_map/slice | solution.py:106
  15.6 1.6 copy.44
  17.2 5.2 %all-to-all-start = ((bf16[8,2,32,1024]{3,2,1,0:T(8,128)(2,1)}), bf16[8,2,32,1024]{3,2,1,0:T(8,128)(2,1)S(1)}, u32[]{:S(2)}, u32[]{:S(2)}) async-start(bf16[8,2,32,1024]{3,2,1,0:T(8,128)(2,1)} %bitcast.40), calls=%async_computation | async-start | bytes 2097152 | tf_op jit(solution)/shard_map/all_to_all | solution.py:108
  22.4 18.5 %all-gather = bf16[8,32,8]{1,2,0:T(8,128)(2,1)S(1)} all-gather(bf16[1,32,8]{1,2,0:T(8,128)(2,1)S(1)} %convert_bitcast_fusion), channel_id=1, replica_groups=mesh['bulk'=4,'z'=4,'core'=2] {'bulk','core'}, dimensions={0}, use_global_device_ids=true | all-gather | bytes 4608 | tf_op jit(solution)/shard_map/all_gather | solution.py:98
  40.9 0.1 reshape.37
  41.0 0.1 copy.20
  41.1 0.3 broadcast_in_dim.4
  41.4 0.9 copy.45
  42.4 7.1 %fusion = (bf16[32,8,4,1024]{3,2,1,0:T(4,128)(2,1)}, bf16[32,8,4,1024]{3,2,1,0:T(4,128)(2,1)S(1)}) fusion(bf16[32,8,16,1024]{3,2,1,0:T(8,128)(2,1)} %bitcast.53), kind=kLoop, calls=%fused_computation.10 | loop fusion | bytes 8388608 | tf_op jit(solution)/shard_map/slice | solution.py:106
  49.5 2.5 copy.42
  52.0 3.7 %all-to-all-start.4 = ((bf16[8,4,32,1024]{3,2,1,0:T(8,128)(2,1)}), bf16[8,4,32,1024]{3,2,1,0:T(8,128)(2,1)S(1)}, u32[]{:S(2)}, u32[]{:S(2)}) async-start(bf16[8,4,32,1024]{3,2,1,0:T(8,128)(2,1)} %bitcast.55), calls=%async_computation.6 | async-start | bytes 4194304 | tf_op jit(solution)/shard_map/all_to_all | solution.py:108
  55.8 0.0 reduce-scatter.5.cloned.1.call-start
  55.8 0.0 all-gather.3.cloned.1.call-done.int_ref
  55.9 1.0 copy-done
  56.9 7.0 %ladder.4 = bf16[4,4,2,2,32,256]{5,4,3,2,1,0:T(8,128)(2,1)} custom-call(bf16[4,2,2,32,1024]{4,3,2,1,0:T(8,128)(2,1)S(1)} %bitcast.43, bf16[128,2048]{1,0:T(8,128)(2,1)S(1)} %bitcast.46, bf16[128,128]{1,0:T(8,128)(2,1)S(1)} %copy-done.3, bf16[2048,2048]{1,0:T(8,128)(2,1)} %all-gather.3.cloned.1.call-done.int_ref), custom_call_target="tpu_custom_call" | custom-call | flops 2281701376 | bytes 10485760 | tf_op jit(solution)/shard_map/ladder/pallas_call | solution.py:60
  63.9 0.0 reduce-scatter.5.cloned.1.call-update
  63.9 0.0 reduce-scatter.9.cloned.1.call-start
  63.9 18.4 %all-to-all-done.4 = bf16[8,4,32,1024]{3,2,1,0:T(8,128)(2,1)S(1)} async-done(((bf16[8,4,32,1024]{3,2,1,0:T(8,128)(2,1)}), bf16[8,4,32,1024]{3,2,1,0:T(8,128)(2,1)S(1)}, u32[]{:S(2)}, u32[]{:S(2)}) %all-to-all-start.4) | async-done | bytes 2097184 | tf_op jit(solution)/shard_map/all_to_all | solution.py:108
  82.3 1.0 copy-done.1
  83.4 9.7 %ladder.6 = bf16[4,4,2,4,32,256]{5,4,3,2,1,0:T(8,128)(2,1)} custom-call(bf16[4,2,4,32,1024]{4,3,2,1,0:T(8,128)(2,1)S(1)} %bitcast.44, bf16[128,2048]{1,0:T(8,128)(2,1)S(1)} %bitcast.47, bf16[128,128]{1,0:T(8,128)(2,1)S(1)} %copy-done.3, bf16[2048,2048]{1,0:T(8,128)(2,1)} %all-gather.3.cloned.1.call-done.int_ref), custom_call_target="tpu_custom_call" | custom-call | flops 4563402752 | bytes 12582912 | tf_op jit(solution)/shard_map/ladder/pallas_call | solution.py:60
  93.1 0.0 reduce-scatter.9.cloned.1.call-update
  93.1 0.2 reduce-scatter.7.cloned.1.call-start
  93.3 1.3 copy-done.4
  94.7 1.2 copy.43
  95.8 29.2 %all_to_all.40 = bf16[8,4,32,1024]{3,2,1,0:T(8,128)(2,1)S(1)} all-to-all(bf16[8,4,32,1024]{3,2,1,0:T(8,128)(2,1)S(1)} %bitcast.57), channel_id=1, replica_groups=mesh['bulk'=4,'z'=4,'core'=2] {'bulk','core'}, dimensions={0} | all-to-all | bytes 4194304 | tf_op jit(solution)/shard_map/all_to_all | solution.py:108
  125.0 9.6 %ladder.5 = bf16[4,4,2,4,32,256]{5,4,3,2,1,0:T(8,128)(2,1)} custom-call(bf16[4,2,4,32,1024]{4,3,2,1,0:T(8,128)(2,1)S(1)} %bitcast.45, bf16[128,2048]{1,0:T(8,128)(2,1)S(1)} %bitcast.48, bf16[128,128]{1,0:T(8,128)(2,1)S(1)} %copy-done.3, bf16[2048,2048]{1,0:T(8,128)(2,1)} %all-gather.3.cloned.1.call-done.int_ref), custom_call_target="tpu_custom_call" | custom-call | flops 4563402752 | bytes 12582912 | tf_op jit(solution)/shard_map/ladder/pallas_call | solution.py:60
  134.7 0.0 reduce-scatter.7.cloned.1.call-update
  134.7 0.0 reduce-scatter.11.cloned.1.call-start
  134.7 3.4 %slice.19 = bf16[32,8,6,1024]{3,2,1,0:T(8,128)(2,1)S(1)} slice(bf16[32,8,16,1024]{3,2,1,0:T(8,128)(2,1)} %bitcast.54), slice={[0:32], [0:8], [10:16], [0:1024]} | slice | bytes 6291456 | tf_op jit(solution)/shard_map/slice | solution.py:106
  138.1 1.8 copy.40
  140.0 41.0 %all_to_all.41 = bf16[8,6,32,1024]{3,2,1,0:T(8,128)(2,1)} all-to-all(bf16[8,6,32,1024]{3,2,1,0:T(8,128)(2,1)S(1)} %bitcast.51), channel_id=1, replica_groups=mesh['bulk'=4,'z'=4,'core'=2] {'bulk','core'}, dimensions={0} | all-to-all | bytes 6291456 | tf_op jit(solution)/shard_map/all_to_all | solution.py:108
  181.0 12.6 %ladder.7 = bf16[4,4,2,6,32,256]{5,4,3,2,1,0:T(8,128)(2,1)} custom-call(bf16[4,2,6,32,1024]{4,3,2,1,0:T(8,128)(2,1)} %bitcast.59, bf16[128,2048]{1,0:T(8,128)(2,1)S(1)} %bitcast.49, bf16[128,128]{1,0:T(8,128)(2,1)S(1)} %copy-done.3, bf16[2048,2048]{1,0:T(8,128)(2,1)} %all-gather.3.cloned.1.call-done.int_ref), custom_call_target="tpu_custom_call" | custom-call | flops 6845104128 | bytes 14680064 | tf_op jit(solution)/shard_map/ladder/pallas_call | solution.py:60
  193.6 0.0 reduce-scatter.5.cloned.1.call-done
  193.6 10.3 %all_to_all.42 = bf16[8,2,32,256]{3,2,1,0:T(8,128)(2,1)S(1)} all-to-all(bf16[8,2,32,256]{3,2,1,0:T(8,128)(2,1)} %bitcast.64), channel_id=1, replica_groups=mesh['bulk'=4,'z'=4,'core'=2] {'bulk','core'}, dimensions={0} | all-to-all | bytes 524288 | tf_op jit(solution)/shard_map/all_to_all | solution.py:114
  203.9 3.5 %all-to-all-start.5 = ((bf16[8,4,32,256]{3,2,1,0:T(8,128)(2,1)}), bf16[8,4,32,256]{3,2,1,0:T(8,128)(2,1)S(1)}, u32[]{:S(2)}, u32[]{:S(2)}) async-start(bf16[8,4,32,256]{3,2,1,0:T(8,128)(2,1)} %bitcast.62), calls=%async_computation.8 | async-start | bytes 1048576 | tf_op jit(solution)/shard_map/all_to_all | solution.py:114
  207.4 0.0 reduce-scatter.7.cloned.1.call-done
  207.4 9.6 %all-to-all-done.5 = bf16[8,4,32,256]{3,2,1,0:T(8,128)(2,1)S(1)} async-done(((bf16[8,4,32,256]{3,2,1,0:T(8,128)(2,1)}), bf16[8,4,32,256]{3,2,1,0:T(8,128)(2,1)S(1)}, u32[]{:S(2)}, u32[]{:S(2)}) %all-to-all-start.5) | async-done | bytes 524320 | tf_op jit(solution)/shard_map/all_to_all | solution.py:114
  217.1 13.1 %all_to_all.43 = bf16[8,4,32,256]{3,2,1,0:T(8,128)(2,1)S(1)} all-to-all(bf16[8,4,32,256]{3,2,1,0:T(8,128)(2,1)} %bitcast.63), channel_id=1, replica_groups=mesh['bulk'=4,'z'=4,'core'=2] {'bulk','core'}, dimensions={0} | all-to-all | bytes 1048576 | tf_op jit(solution)/shard_map/all_to_all | solution.py:114
  230.2 23.2 %reduce-scatter.11.cloned.1.call-done = bf16[1,4,2,6,32,256]{5,4,3,2,1,0:T(8,128)(2,1)} async-done(((bf16[4,4,2,6,32,256]{5,4,3,2,1,0:T(8,128)(2,1)}), bf16[1,4,2,6,32,256]{5,4,3,2,1,0:T(8,128)(2,1)}) %reduce-scatter.11.cloned.1.call-update) | async-done | bytes 786448 | tf_op jit(solution)/shard_map/reduce_scatter | solution.py:111
  253.4 16.2 %all_to_all.44 = bf16[8,6,32,256]{3,2,1,0:T(8,128)(2,1)S(1)} all-to-all(bf16[8,6,32,256]{3,2,1,0:T(8,128)(2,1)} %bitcast.61), channel_id=1, replica_groups=mesh['bulk'=4,'z'=4,'core'=2] {'bulk','core'}, dimensions={0} | all-to-all | bytes 1572864 | tf_op jit(solution)/shard_map/all_to_all | solution.py:114
  269.6 0.2 pad_maximum_fusion
  269.9 4.0 %copy.24 = bf16[128,32,256]{0,1,2:T(8,128)(2,1)} copy(bf16[128,32,256]{2,1,0:T(8,128)(2,1)S(1)} %bitcast.56) | data formatting | bytes 4194304 | tf_op jit(solution)/shard_map/reshape | solution.py:116
  273.9 3.9 %copy.41 = bf16[32,8,32,128]{3,1,2,0:T(8,128)(2,1)} copy(bf16[32,8,32,128]{3,2,1,0:T(8,128)(2,1)} %bitcast.58) | data formatting | bytes 4194304
  (16 shorter events, 0.1 us)
Async XLA Ops:
  6.5 49.3 %all-gather.3.cloned.1.call-start = ((), (), s32[]{:S(2)}) async-start(), calls=%async_computation.12 | async-start | bytes 12582912 | tf_op jit(solution)/shard_map/all_gather | solution.py:97
  7.2 2.2 copy-start.5
  15.6 6.8 %copy-start.6 = (s32[32,8]{0,1:T(8,128)S(1)}, s32[32,8]{0,1:T(8,128)}, u32[]{:S(2)}) copy-start(s32[32,8]{0,1:T(8,128)} %param.6) | copy-start | bytes 3076
  17.2 34.8 %all-to-all-start = ((bf16[8,2,32,1024]{3,2,1,0:T(8,128)(2,1)}), bf16[8,2,32,1024]{3,2,1,0:T(8,128)(2,1)S(1)}, u32[]{:S(2)}, u32[]{:S(2)}) async-start(bf16[8,2,32,1024]{3,2,1,0:T(8,128)(2,1)} %bitcast.40), calls=%async_computation | async-start | bytes 2097152 | tf_op jit(solution)/shard_map/all_to_all | solution.py:108
  52.0 3.8 %copy-start.3 = (bf16[128,128]{1,0:T(8,128)(2,1)S(1)}, bf16[128,128]{1,0:T(8,128)(2,1)}, u32[]{:S(2)}) copy-start(bf16[128,128]{1,0:T(8,128)(2,1)} %occ_ref.7) | copy-start | bytes 98308
  52.0 30.3 %all-to-all-start.4 = ((bf16[8,4,32,1024]{3,2,1,0:T(8,128)(2,1)}), bf16[8,4,32,1024]{3,2,1,0:T(8,128)(2,1)S(1)}, u32[]{:S(2)}, u32[]{:S(2)}) async-start(bf16[8,4,32,1024]{3,2,1,0:T(8,128)(2,1)} %bitcast.55), calls=%async_computation.6 | async-start | bytes 4194304 | tf_op jit(solution)/shard_map/all_to_all | solution.py:108
  55.8 137.9 %reduce-scatter.5.cloned.1.call-start = ((), (), s32[]{:S(2)}) async-start(), calls=%async_computation.13 | async-start | bytes 1310720 | tf_op jit(solution)/shard_map/reduce_scatter | solution.py:111
  55.9 1.0 copy-start
  63.9 140.0 %reduce-scatter.9.cloned.1.call-start = ((), (), s32[]{:S(2)}) async-start(), calls=%async_computation.15 | async-start | bytes 2621440 | tf_op jit(solution)/shard_map/reduce_scatter | solution.py:111
  82.3 1.0 copy-start.1
  93.1 1.6 copy-start.4
  93.1 114.3 %reduce-scatter.7.cloned.1.call-start = ((), (), s32[]{:S(2)}) async-start(), calls=%async_computation.14 | async-start | bytes 2621440 | tf_op jit(solution)/shard_map/reduce_scatter | solution.py:111
  95.8 29.2 %copy-start.2 = (bf16[16,8,16,128]{3,1,2,0:T(8,128)(2,1)S(1)}, bf16[16,8,16,128]{3,1,2,0:T(8,128)(2,1)}, u32[]{:S(2)}) copy-start(bf16[16,8,16,128]{3,1,2,0:T(8,128)(2,1)} %copy.45) | copy-start | bytes 1572868
  134.7 118.7 %reduce-scatter.11.cloned.1.call-start = ((), (), s32[]{:S(2)}) async-start(), calls=%async_computation.16 | async-start | bytes 3932160 | tf_op jit(solution)/shard_map/reduce_scatter | solution.py:111
  203.9 13.2 %all-to-all-start.5 = ((bf16[8,4,32,256]{3,2,1,0:T(8,128)(2,1)}), bf16[8,4,32,256]{3,2,1,0:T(8,128)(2,1)S(1)}, u32[]{:S(2)}, u32[]{:S(2)}) async-start(bf16[8,4,32,256]{3,2,1,0:T(8,128)(2,1)} %bitcast.62), calls=%async_computation.8 | async-start | bytes 1048576 | tf_op jit(solution)/shard_map/all_to_all | solution.py:114
Sparse Core Ops, SparseCore 0:
  12.4 22.5 all-gather.2
  64.0 28.6 reduce-scatter.4
  95.2 42.5 reduce-scatter.8
  139.9 43.1 reduce-scatter.6
  193.7 59.6 reduce-scatter.10

commit v3 on v2

--- a/solution.py
+++ b/solution.py
@@ -79,11 +79,12 @@
 
 
 def chunk_sizes(seconds):
-    if seconds % 16 == 0:
-        unit = seconds // 16
-        return [2 * unit, 4 * unit, 4 * unit, 6 * unit]
-    pieces = min(4, seconds)
-    return [seconds // pieces] * (pieces - 1) + [seconds - seconds // pieces * (pieces - 1)]
+    if seconds % 8 == 0:
+        unit = seconds // 8
+        return [2 * unit, 3 * unit, 3 * unit]
+    pieces = min(3, seconds)
+    first = seconds // pieces
+    return [first] * (pieces - 1) + [seconds - first * (pieces - 1)]
 
 
 def shards(amplitudes, amp_tiles, occ_coupling, integrals, int_tiles):
@@ -93,26 +94,37 @@
     peers = lax.axis_size("bulk")
     cores = lax.axis_size("core")
     owners = lax.axis_size("z")
-    second_dev = occ_all // (peers * cores)
+    group = peers * cores
+    second_dev = occ_all // group
+    swap = functools.partial(
+        lax.all_to_all, axis_name=GROUP, split_axis=0, concat_axis=0, tiled=True
+    )
+    by_owner = amplitudes.reshape(first_dev, group, second_dev, local_cols)
+    sizes = chunk_sizes(second_dev)
+    sent = []
+    begin = 0
+    for step in sizes:
+        sent.append(by_owner[:, :, begin : begin + step].transpose(1, 2, 0, 3))
+        begin += step
+    tiles = amp_tiles.astype(jnp.bfloat16)
+    tiles_all = swap(jnp.broadcast_to(tiles[None], (group,) + tiles.shape))
+    tiles_all, first = lax.optimization_barrier((tiles_all, sent[0]))
+    arrived = swap(first)
     int_kept = lax.all_gather(keep_tiles(integrals, int_tiles), "core", axis=0, tiled=True)
-    tiles_all = lax.all_gather(amp_tiles.astype(jnp.bfloat16), GROUP, axis=0, tiled=True)
     tiles_all = tiles_all.reshape(peers, cores, first_dev, local_cols // TILE)
     tiles_all = tiles_all.transpose(0, 2, 1, 3).reshape(occ_all, cores * (local_cols // TILE))
     mask = jnp.repeat(tiles_all, TILE, axis=1)
-    by_owner = amplitudes.reshape(first_dev, peers * cores, second_dev, local_cols)
     finished = []
-    begin = 0
-    for step in chunk_sizes(second_dev):
-        sent = by_owner[:, :, begin : begin + step].transpose(1, 2, 0, 3)
-        begin += step
-        arrived = lax.all_to_all(sent, GROUP, split_axis=0, concat_axis=0, tiled=True)
+    for at, step in enumerate(sizes):
+        if at + 1 < len(sizes):
+            arrived, ready = lax.optimization_barrier((arrived, sent[at + 1]))
+            following = swap(ready)
         arrived = arrived.reshape(peers, cores, step, first_dev, local_cols)
         partial = ladder(arrived, mask, occ_coupling, int_kept, owners)
         total = lax.psum_scatter(partial, "z", scatter_dimension=0, tiled=False)
         width = total.shape[-1]
-        total = total.reshape(peers * cores, step, first_dev, width)
-        back = lax.all_to_all(total, GROUP, split_axis=0, concat_axis=0, tiled=True)
-        finished.append(back)
+        finished.append(swap(total.reshape(group, step, first_dev, width)))
+        arrived = following
     joined = jnp.concatenate(finished, axis=1).reshape(occ_all, first_dev, width)
     return joined.transpose(2, 1, 0).reshape(width, local_rows)
 

time: 285 us -> 274 us (0.961)
  blocking collectives: 128 us -> 71.7 us
  waiting for transfers between devices: 51.4 us -> 96.6 us
  starting transfers between devices: 12.7 us -> 17.8 us
  Pallas kernels: 38.9 us -> 34.7 us
    all_to_all x5 -> x3, blocking collectives: 110 us -> 71.7 us  [the longest x1 42.3 us: shards(): following = swap(ready)]
    reduce_scatter x4 -> x3, waiting for transfers between devices: 23.2 us -> 50.9 us  [shards(): total = lax.psum_scatter(partial, 'z', scatter_dimension=0, tiled=False)]
    all_gather x1 -> x0, blocking collectives: 18.5 us -> none  [shards(): lax.all_gather(amp_tiles.astype(jnp.bfloat16), GROUP, axis=0, tiled=True)]
    all_to_all x3 -> x4, waiting for transfers between devices: 28.1 us -> 45.7 us  [the longest x1 31.6 us: shards(): following = swap(ready)]
    all_to_all x3 -> x4, starting transfers between devices: 12.4 us -> 17.5 us  [the longest x1 5.17 us: shards(): tiles_all = swap(jnp.broadcast_to(tiles[None], (group,) + tiles.shape))]
    pallas_call x4 -> x3, Pallas kernels: 38.9 us -> 34.7 us  [ladder(): pl.pallas_call(functools.partial(ladder_kernel, rows_at), grid=(seconds /...]
    slice x3 -> x2, local copies, waits for them, and re-layouts: 13.8 us -> 11.7 us  [shards(): sent.append(by_owner[:, :, begin:begin + step].transpose(1, 2, 0, 3))]
    unnamed x20 -> x14, local copies, waits for them, and re-layouts: 16.9 us -> 18.2 us
  transfers between devices with their start and end apart: 8 -> 8, of which waited for: 3 -> 3; matrix products, arithmetic and copies ran while one was open for 8% -> 9% of each run, Pallas kernels for 14% -> 9%
where the time goes in v3:
time: 274 us; the launch traced here: 273 us
  waiting for transfers between devices  96.6 us (35%)
  blocking collectives  71.7 us (26%)
  local copies, waits for them, and re-layouts  35.1 us (13%)
  Pallas kernels  34.7 us (13%)
  starting transfers between devices  17.8 us (6%)
  between operations  13.2 us (5%)
  other arithmetic  3.9 us (1%)
    reduce_scatter x3, waiting for transfers between devices, shards(): total = lax.psum_scatter(partial, 'z', scatter_dimension=0, tiled=False)  50.9 us
    all_to_all x1, blocking collectives, shards(): following = swap(ready)  42.3 us
    pallas_call x3, Pallas kernels, ladder(): pl.pallas_call(functools.partial(ladder_kernel, rows_at), grid=(seconds /...  34.7 us
    all_to_all x1, waiting for transfers between devices, shards(): following = swap(ready)  31.6 us
    all_to_all x2, blocking collectives, shards(): finished.append(swap(total.reshape(group, step, first_dev, width)))  29.4 us
    unnamed x14, local copies, waits for them, and re-layouts  18.2 us
    all_to_all x1, waiting for transfers between devices, shards(): arrived = swap(first)  14.1 us
    slice x2, local copies, waits for them, and re-layouts, shards(): sent.append(by_owner[:, :, begin:begin + step].transpose(1, 2, 0, 3))  11.7 us
  transfers between devices with their start and end apart: 8, of which 3 were waited for; matrix products, arithmetic and copies ran while one was open for 9% of the time, Pallas kernels for 9%

profile of v3, /device:TPU:0, one launch (start us, length us, event | category | flops | bytes accessed | tf_op | source)
XLA Modules:
  0.0 273.0 jit_solution(3280364066495263270)
XLA Ops:
  6.5 0.0 all-gather.2.cloned.1.call-start
  6.5 0.0 copy-start.1
  6.5 0.8 convert_element_type.7
  7.4 0.6 mul.11
  8.0 0.7 copy-done.1
  8.7 2.8 %bitcast_multiply_fusion = bf16[1024,2048]{1,0:T(8,128)(2,1)} fusion(bf16[1024,2048]{1,0:T(8,128)(2,1)S(1)} %copy-done.1, bf16[128,8,16,128]{3,2,1,0:T(8,128)(2,1)S(1)} %bitcast.42), kind=kLoop, calls=%fused_computation | loop fusion | flops 2097152 | bytes 12582912 | tf_op jit(solution)/shard_map/mul | solution.py:18
  11.6 0.0 copy-start.2
  11.6 0.0 all-gather.2.cloned.1.call-update
  11.6 0.7 copy-done.2
  12.3 0.7 reshape.41
  13.0 5.2 %all-to-all-start = ((bf16[8,2,128]{2,1,0:T(2,128)(2,1)}), bf16[8,2,128]{2,1,0:T(2,128)(2,1)S(1)}, u32[]{:S(2)}, u32[]{:S(2)}) async-start(bf16[8,2,128]{2,1,0:T(2,128)(2,1)} %reshape.41), calls=%async_computation | async-start | bytes 8192 | tf_op jit(solution)/shard_map/all_to_all | solution.py:110
  18.1 3.4 %slice.12 = bf16[32,8,4,1024]{3,2,1,0:T(4,128)(2,1)S(1)} slice(bf16[32,8,16,1024]{3,2,1,0:T(8,128)(2,1)} %bitcast.43), slice={[0:32], [0:8], [0:4], [0:1024]} | slice | bytes 4194304 | tf_op jit(solution)/shard_map/slice | solution.py:107
  21.5 2.5 copy.32
  24.0 0.0 all-to-all-done
  24.0 0.1 reshape.42
  24.1 4.3 %all-to-all-start.1 = ((bf16[8,4,32,1024]{3,2,1,0:T(8,128)(2,1)}), bf16[8,4,32,1024]{3,2,1,0:T(8,128)(2,1)S(1)}, u32[]{:S(2)}, u32[]{:S(2)}) async-start(bf16[8,4,32,1024]{3,2,1,0:T(8,128)(2,1)} %bitcast.47), calls=%async_computation.1 | async-start | bytes 4194304 | tf_op jit(solution)/shard_map/all_to_all | solution.py:112
  28.4 0.0 reduce-scatter.4.cloned.1.call-start
  28.4 8.4 %fusion = (bf16[32,8,6,1024]{3,2,1,0:T(8,128)(2,1)}, bf16[32,8,6,1024]{3,2,1,0:T(8,128)(2,1)S(1)}) fusion(bf16[32,8,16,1024]{3,2,1,0:T(8,128)(2,1)} %bitcast.44), kind=kLoop, calls=%fused_computation.7 | loop fusion | bytes 12582912 | tf_op jit(solution)/shard_map/slice | solution.py:107
  36.8 0.0 copy-start
  36.8 3.5 %copy.30 = bf16[32,8,6,1024]{3,0,2,1:T(8,128)(2,1)} copy(bf16[32,8,6,1024]{3,2,1,0:T(8,128)(2,1)S(1)} %get-tuple-element.18) | data formatting | bytes 6291456
  40.3 0.1 reshape.35
  40.3 0.1 copy.14
  40.5 0.3 broadcast_in_dim.5
  40.8 0.1 copy.33
  41.0 14.1 %all-to-all-done.1 = bf16[8,4,32,1024]{3,2,1,0:T(8,128)(2,1)S(1)} async-done(((bf16[8,4,32,1024]{3,2,1,0:T(8,128)(2,1)}), bf16[8,4,32,1024]{3,2,1,0:T(8,128)(2,1)S(1)}, u32[]{:S(2)}, u32[]{:S(2)}) %all-to-all-start.1) | async-done | bytes 2097184 | tf_op jit(solution)/shard_map/all_to_all | solution.py:112
  55.0 0.0 copy-done
  55.0 9.6 %ladder.3 = bf16[4,4,2,4,32,256]{5,4,3,2,1,0:T(8,128)(2,1)} custom-call(bf16[4,2,4,32,1024]{4,3,2,1,0:T(8,128)(2,1)S(1)} %bitcast.38, bf16[128,2048]{1,0:T(8,128)(2,1)S(1)} %bitcast.39, bf16[128,128]{1,0:T(8,128)(2,1)S(1)} %copy-done, bf16[2048,2048]{1,0:T(8,128)(2,1)} %all-gather.2.cloned.1.call-done.int_ref), custom_call_target="tpu_custom_call" | custom-call | flops 4563402752 | bytes 12582912 | tf_op jit(solution)/shard_map/ladder/pallas_call | solution.py:60
  64.7 0.0 reduce-scatter.4.cloned.1.call-update
  64.7 4.5 %all-to-all-start.3 = ((bf16[8,6,32,1024]{3,2,1,0:T(8,128)(2,1)}), bf16[8,6,32,1024]{3,2,1,0:T(8,128)(2,1)}, u32[]{:S(2)}, u32[]{:S(2)}) async-start(bf16[8,6,32,1024]{3,2,1,0:T(8,128)(2,1)} %bitcast.45), calls=%async_computation.4 | async-start | bytes 6291456 | tf_op jit(solution)/shard_map/all_to_all | solution.py:121
  69.2 0.2 reduce-scatter.6.cloned.1.call-start
  69.4 6.0 %copy.29 = bf16[32,8,6,1024]{3,0,2,1:T(8,128)(2,1)} copy(bf16[32,8,6,1024]{3,2,1,0:T(8,128)(2,1)} %get-tuple-element.17) | data formatting | bytes 6291456
  75.4 31.6 %all-to-all-done.3 = bf16[8,6,32,1024]{3,2,1,0:T(8,128)(2,1)} async-done(((bf16[8,6,32,1024]{3,2,1,0:T(8,128)(2,1)}), bf16[8,6,32,1024]{3,2,1,0:T(8,128)(2,1)}, u32[]{:S(2)}, u32[]{:S(2)}) %all-to-all-start.3) | async-done | bytes 3145760 | tf_op jit(solution)/shard_map/all_to_all | solution.py:121
  107.1 12.6 %ladder.4 = bf16[4,4,2,6,32,256]{5,4,3,2,1,0:T(8,128)(2,1)} custom-call(bf16[4,2,6,32,1024]{4,3,2,1,0:T(8,128)(2,1)} %bitcast.8.amp_ref, bf16[128,2048]{1,0:T(8,128)(2,1)S(1)} %bitcast.40, bf16[128,128]{1,0:T(8,128)(2,1)S(1)} %copy-done, bf16[2048,2048]{1,0:T(8,128)(2,1)} %all-gather.2.cloned.1.call-done.int_ref), custom_call_target="tpu_custom_call" | custom-call | flops 6845104128 | bytes 14680064 | tf_op jit(solution)/shard_map/ladder/pallas_call | solution.py:60
  119.6 0.0 reduce-scatter.6.cloned.1.call-update
  119.6 0.0 reduce-scatter.8.cloned.1.call-start
  119.7 42.3 %all_to_all.35 = bf16[8,6,32,1024]{3,2,1,0:T(8,128)(2,1)} all-to-all(bf16[8,6,32,1024]{3,2,1,0:T(8,128)(2,1)} %bitcast.46), channel_id=1, replica_groups=mesh['bulk'=4,'z'=4,'core'=2] {'bulk','core'}, dimensions={0} | all-to-all | bytes 6291456 | tf_op jit(solution)/shard_map/all_to_all | solution.py:121
  162.0 12.5 %ladder.5 = bf16[4,4,2,6,32,256]{5,4,3,2,1,0:T(8,128)(2,1)} custom-call(bf16[4,2,6,32,1024]{4,3,2,1,0:T(8,128)(2,1)} %bitcast.50, bf16[128,2048]{1,0:T(8,128)(2,1)S(1)} %bitcast.41, bf16[128,128]{1,0:T(8,128)(2,1)S(1)} %copy-done, bf16[2048,2048]{1,0:T(8,128)(2,1)} %all-gather.2.cloned.1.call-done.int_ref), custom_call_target="tpu_custom_call" | custom-call | flops 6845104128 | bytes 14680064 | tf_op jit(solution)/shard_map/ladder/pallas_call | solution.py:60
  174.5 0.0 reduce-scatter.8.cloned.1.call-update
  174.6 0.0 reduce-scatter.4.cloned.1.call-done
  174.6 13.2 %all_to_all.36 = bf16[8,4,32,256]{3,2,1,0:T(8,128)(2,1)S(1)} all-to-all(bf16[8,4,32,256]{3,2,1,0:T(8,128)(2,1)} %bitcast.54), channel_id=1, replica_groups=mesh['bulk'=4,'z'=4,'core'=2] {'bulk','core'}, dimensions={0} | all-to-all | bytes 1048576 | tf_op jit(solution)/shard_map/all_to_all | solution.py:126
  187.7 0.0 reduce-scatter.6.cloned.1.call-done
  187.7 3.5 %all-to-all-start.4 = ((bf16[8,6,32,256]{3,2,1,0:T(8,128)(2,1)}), bf16[8,6,32,256]{3,2,1,0:T(8,128)(2,1)S(1)}, u32[]{:S(2)}, u32[]{:S(2)}) async-start(bf16[8,6,32,256]{3,2,1,0:T(8,128)(2,1)} %bitcast.52), calls=%async_computation.6 | async-start | bytes 1572864 | tf_op jit(solution)/shard_map/all_to_all | solution.py:126
  191.3 50.8 %reduce-scatter.8.cloned.1.call-done = bf16[1,4,2,6,32,256]{5,4,3,2,1,0:T(8,128)(2,1)} async-done(((bf16[4,4,2,6,32,256]{5,4,3,2,1,0:T(8,128)(2,1)}), bf16[1,4,2,6,32,256]{5,4,3,2,1,0:T(8,128)(2,1)}) %reduce-scatter.8.cloned.1.call-update) | async-done | bytes 786448 | tf_op jit(solution)/shard_map/reduce_scatter | solution.py:124
  242.1 0.0 all-to-all-done.4
  242.1 16.2 %all_to_all.37 = bf16[8,6,32,256]{3,2,1,0:T(8,128)(2,1)S(1)} all-to-all(bf16[8,6,32,256]{3,2,1,0:T(8,128)(2,1)} %bitcast.53), channel_id=1, replica_groups=mesh['bulk'=4,'z'=4,'core'=2] {'bulk','core'}, dimensions={0} | all-to-all | bytes 1572864 | tf_op jit(solution)/shard_map/all_to_all | solution.py:126
  258.3 0.2 pad_maximum_fusion
  258.6 4.0 %copy.16 = bf16[128,32,256]{0,1,2:T(8,128)(2,1)} copy(bf16[128,32,256]{2,1,0:T(8,128)(2,1)S(1)} %bitcast.48) | data formatting | bytes 4194304 | tf_op jit(solution)/shard_map/reshape | solution.py:128
  262.6 3.9 %copy.31 = bf16[32,8,32,128]{3,1,2,0:T(8,128)(2,1)} copy(bf16[32,8,32,128]{3,2,1,0:T(8,128)(2,1)} %bitcast.49) | data formatting | bytes 4194304
  (4 shorter events, 0.0 us)
Async XLA Ops:
  6.5 48.5 %all-gather.2.cloned.1.call-start = ((), (), s32[]{:S(2)}) async-start(), calls=%async_computation.10 | async-start | bytes 12582912 | tf_op jit(solution)/shard_map/all_gather | solution.py:113
  6.5 2.2 copy-start.1
  11.6 0.7 copy-start.2
  13.0 11.0 %all-to-all-start = ((bf16[8,2,128]{2,1,0:T(2,128)(2,1)}), bf16[8,2,128]{2,1,0:T(2,128)(2,1)S(1)}, u32[]{:S(2)}, u32[]{:S(2)}) async-start(bf16[8,2,128]{2,1,0:T(2,128)(2,1)} %reshape.41), calls=%async_computation | async-start | bytes 8192 | tf_op jit(solution)/shard_map/all_to_all | solution.py:110
  24.1 30.9 %all-to-all-start.1 = ((bf16[8,4,32,1024]{3,2,1,0:T(8,128)(2,1)}), bf16[8,4,32,1024]{3,2,1,0:T(8,128)(2,1)S(1)}, u32[]{:S(2)}, u32[]{:S(2)}) async-start(bf16[8,4,32,1024]{3,2,1,0:T(8,128)(2,1)} %bitcast.47), calls=%async_computation.1 | async-start | bytes 4194304 | tf_op jit(solution)/shard_map/all_to_all | solution.py:112
  28.4 146.2 %reduce-scatter.4.cloned.1.call-start = ((), (), s32[]{:S(2)}) async-start(), calls=%async_computation.11 | async-start | bytes 2621440 | tf_op jit(solution)/shard_map/reduce_scatter | solution.py:124
  36.8 18.3 %copy-start = (bf16[128,128]{1,0:T(8,128)(2,1)S(1)}, bf16[128,128]{1,0:T(8,128)(2,1)}, u32[]{:S(2)}) copy-start(bf16[128,128]{1,0:T(8,128)(2,1)} %occ_ref.5) | copy-start | bytes 98308
  64.7 42.4 %all-to-all-start.3 = ((bf16[8,6,32,1024]{3,2,1,0:T(8,128)(2,1)}), bf16[8,6,32,1024]{3,2,1,0:T(8,128)(2,1)}, u32[]{:S(2)}, u32[]{:S(2)}) async-start(bf16[8,6,32,1024]{3,2,1,0:T(8,128)(2,1)} %bitcast.45), calls=%async_computation.4 | async-start | bytes 6291456 | tf_op jit(solution)/shard_map/all_to_all | solution.py:121
  69.2 118.6 %reduce-scatter.6.cloned.1.call-start = ((), (), s32[]{:S(2)}) async-start(), calls=%async_computation.12 | async-start | bytes 3932160 | tf_op jit(solution)/shard_map/reduce_scatter | solution.py:124
  119.6 122.5 %reduce-scatter.8.cloned.1.call-start = ((), (), s32[]{:S(2)}) async-start(), calls=%async_computation.13 | async-start | bytes 3932160 | tf_op jit(solution)/shard_map/reduce_scatter | solution.py:124
  187.7 54.4 %all-to-all-start.4 = ((bf16[8,6,32,256]{3,2,1,0:T(8,128)(2,1)}), bf16[8,6,32,256]{3,2,1,0:T(8,128)(2,1)S(1)}, u32[]{:S(2)}, u32[]{:S(2)}) async-start(bf16[8,6,32,256]{3,2,1,0:T(8,128)(2,1)} %bitcast.52), calls=%async_computation.6 | async-start | bytes 1572864 | tf_op jit(solution)/shard_map/all_to_all | solution.py:126
Sparse Core Ops, SparseCore 0:
  11.7 22.9 all-gather.1
  64.8 43.3 reduce-scatter.3
  119.8 59.7 reduce-scatter.5
  181.8 60.2 reduce-scatter.7

commit v4 on v3

--- a/solution.py
+++ b/solution.py
@@ -27,7 +27,7 @@
     for at in range(rows_at):
         halves = []
         for core in range(cores):
-            mask = mask_ref[:, core * cols : (core + 1) * cols]
+            mask = jnp.concatenate([mask_ref[src, core] for src in range(peers)], axis=0)
             pieces = [amp_ref[src, core, at] for src in range(peers)]
             slab = jnp.concatenate(pieces, axis=0) * mask
             mixed = jnp.dot(occ, slab, preferred_element_type=jnp.float32)
@@ -62,7 +62,7 @@
         grid=(seconds // rows_at,),
         in_specs=[
             pl.BlockSpec((peers, cores, rows_at, firsts, cols), lambda g: (0, 0, g, 0, 0)),
-            pl.BlockSpec((occ_all, depth), lambda g: (0, 0)),
+            pl.BlockSpec((peers, cores, firsts, cols), lambda g: (0, 0, 0, 0)),
             pl.BlockSpec((occ_all, occ_all), lambda g: (0, 0)),
             pl.BlockSpec((depth, total), lambda g: (0, 0), pipeline_mode=pl.Buffered(1)),
         ],
@@ -87,6 +87,19 @@
     return [first] * (pieces - 1) + [seconds - first * (pieces - 1)]
 
 
+def gather_maps(spread, peers, cores):
+    swapped = lax.ppermute(spread, "core", [(at, 1 - at) for at in range(cores)])
+    first = lax.axis_index("core") == 0
+    pair = jnp.stack([jnp.where(first, spread, swapped), jnp.where(first, swapped, spread)])
+    shifts = [pair] + [
+        lax.ppermute(pair, "bulk", [(at, (at + shift) % peers) for at in range(peers)])
+        for shift in range(1, peers)
+    ]
+    doubled = jnp.stack(shifts[::-1] + shifts[::-1])
+    start = lax.rem(2 * peers - 1 - lax.axis_index("bulk"), peers)
+    return lax.dynamic_slice_in_dim(doubled, start, peers, axis=0)
+
+
 def shards(amplitudes, amp_tiles, occ_coupling, integrals, int_tiles):
     local_rows, local_cols = amplitudes.shape
     occ_all = occ_coupling.shape[0]
@@ -106,14 +119,9 @@
     for step in sizes:
         sent.append(by_owner[:, :, begin : begin + step].transpose(1, 2, 0, 3))
         begin += step
-    tiles = amp_tiles.astype(jnp.bfloat16)
-    tiles_all = swap(jnp.broadcast_to(tiles[None], (group,) + tiles.shape))
-    tiles_all, first = lax.optimization_barrier((tiles_all, sent[0]))
-    arrived = swap(first)
+    arrived = swap(sent[0])
     int_kept = lax.all_gather(keep_tiles(integrals, int_tiles), "core", axis=0, tiled=True)
-    tiles_all = tiles_all.reshape(peers, cores, first_dev, local_cols // TILE)
-    tiles_all = tiles_all.transpose(0, 2, 1, 3).reshape(occ_all, cores * (local_cols // TILE))
-    mask = jnp.repeat(tiles_all, TILE, axis=1)
+    mask = gather_maps(jnp.repeat(amp_tiles.astype(jnp.bfloat16), TILE, axis=1), peers, cores)
     finished = []
     for at, step in enumerate(sizes):
         if at + 1 < len(sizes):

time: 274 us -> 301 us (1.099)
  waiting for transfers between devices: 96.6 us -> 120 us
    reduce_scatter x3, waiting for transfers between devices: 50.9 us -> 92.9 us  [shards(): total = lax.psum_scatter(partial, 'z', scatter_dimension=0, tiled=False)]
    all_to_all x1, waiting for transfers between devices: 31.6 us -> 21 us  [shards(): following = swap(ready)]
    all_to_all x2 -> x1, waiting for transfers between devices: 14.1 us -> 4.69 us  [shards(): arrived = swap(sent[0])]
    ppermute x0 -> x4, starting transfers between devices: none -> 5.89 us  [the longest x3 5.32 us: gather_maps(): lax.ppermute(pair, 'bulk', [(at, (at + shift) % peers) for at in range(pe...]
    all_to_all x2 -> x1, starting transfers between devices: 9.46 us -> 5.3 us  [shards(): arrived = swap(sent[0])]
    unnamed x14 -> x19, local copies, waits for them, and re-layouts: 18.2 us -> 19.9 us
  transfers between devices with their start and end apart: 8 -> 11, of which waited for: 3 -> 6; matrix products, arithmetic and copies ran while one was open for 9% -> 9% of each run, Pallas kernels for 9% -> 11%
where the time goes in v4:
time: 301 us; the launch traced here: 300 us
  waiting for transfers between devices  120 us (40%)
  blocking collectives  71.7 us (24%)
  local copies, waits for them, and re-layouts  37.7 us (13%)
  Pallas kernels  33.9 us (11%)
  starting transfers between devices  19.6 us (7%)
  between operations  13.3 us (4%)
  other arithmetic  3.95 us (1%)
    reduce_scatter x3, waiting for transfers between devices, shards(): total = lax.psum_scatter(partial, 'z', scatter_dimension=0, tiled=False)  92.9 us
    all_to_all x1, blocking collectives, shards(): following = swap(ready)  42.3 us
    pallas_call x3, Pallas kernels, ladder(): pl.pallas_call(functools.partial(ladder_kernel, rows_at), grid=(seconds /...  33.9 us
    all_to_all x2, blocking collectives, shards(): finished.append(swap(total.reshape(group, step, first_dev, width)))  29.4 us
    all_to_all x1, waiting for transfers between devices, shards(): following = swap(ready)  21 us
    unnamed x19, local copies, waits for them, and re-layouts  19.9 us
    slice x2, local copies, waits for them, and re-layouts, shards(): sent.append(by_owner[:, :, begin:begin + step].transpose(1, 2, 0, 3))  13 us
  transfers between devices with their start and end apart: 11, of which 6 were waited for; matrix products, arithmetic and copies ran while one was open for 9% of the time, Pallas kernels for 11%

profile of v4, /device:TPU:0, one launch (start us, length us, event | category | flops | bytes accessed | tf_op | source)
XLA Modules:
  0.0 300.3 jit_solution(13171991859085468532)
XLA Ops:
  6.5 0.8 convert_element_type.7
  7.4 0.6 mul.11
  8.0 0.7 copy-done.2
  8.7 2.8 bitcast_multiply_fusion
  11.6 0.0 all-gather.2.cloned.1.call-update
  11.6 3.3 %slice.12 = bf16[32,8,4,1024]{3,2,1,0:T(4,128)(2,1)S(1)} slice(bf16[32,8,16,1024]{3,2,1,0:T(8,128)(2,1)} %bitcast.52), slice={[0:32], [0:8], [0:4], [0:1024]} | slice | bytes 4194304 | tf_op jit(solution)/shard_map/slice | solution.py:120
  14.9 2.5 copy.30
  17.4 5.3 %all-to-all-start = ((bf16[8,4,32,1024]{3,2,1,0:T(8,128)(2,1)}), bf16[8,4,32,1024]{3,2,1,0:T(8,128)(2,1)S(1)}, u32[]{:S(2)}, u32[]{:S(2)}) async-start(bf16[8,4,32,1024]{3,2,1,0:T(8,128)(2,1)} %bitcast.56), calls=%async_computation | async-start | bytes 4194304 | tf_op jit(solution)/shard_map/all_to_all | solution.py:122
  22.7 0.1 copy.8
  22.8 0.1 broadcast_in_dim.4
  22.9 0.6 collective-permute-start
  23.5 0.9 collective-permute-done
  24.4 2.8 collective-permute-start.1
  27.3 9.7 %fusion = (bf16[32,8,6,1024]{3,2,1,0:T(8,128)(2,1)}, bf16[32,8,6,1024]{3,2,1,0:T(8,128)(2,1)}) fusion(bf16[32,8,16,1024]{3,2,1,0:T(8,128)(2,1)} %bitcast.53), kind=kLoop, calls=%fused_computation.19 | loop fusion | bytes 12582912 | tf_op jit(solution)/shard_map/slice | solution.py:120
  37.0 5.7 %copy.28 = bf16[32,8,6,1024]{3,0,2,1:T(8,128)(2,1)} copy(bf16[32,8,6,1024]{3,2,1,0:T(8,128)(2,1)} %get-tuple-element.14) | data formatting | bytes 6291456
  42.7 1.0 collective-permute-start.2
  43.6 1.5 collective-permute-start.3
  45.2 4.7 %all-to-all-done = bf16[8,4,32,1024]{3,2,1,0:T(8,128)(2,1)S(1)} async-done(((bf16[8,4,32,1024]{3,2,1,0:T(8,128)(2,1)}), bf16[8,4,32,1024]{3,2,1,0:T(8,128)(2,1)S(1)}, u32[]{:S(2)}, u32[]{:S(2)}) %all-to-all-start) | async-done | bytes 2097184 | tf_op jit(solution)/shard_map/all_to_all | solution.py:122
  49.9 4.4 %all-to-all-start.2 = ((bf16[8,6,32,1024]{3,2,1,0:T(8,128)(2,1)}), bf16[8,6,32,1024]{3,2,1,0:T(8,128)(2,1)}, u32[]{:S(2)}, u32[]{:S(2)}) async-start(bf16[8,6,32,1024]{3,2,1,0:T(8,128)(2,1)} %bitcast.54), calls=%async_computation.3 | async-start | bytes 6291456 | tf_op jit(solution)/shard_map/all_to_all | solution.py:129
  54.3 0.0 copy-start.1
  54.3 0.0 reduce-scatter.4.cloned.1.call-start
  54.4 0.0 collective-permute-done.1
  54.4 0.0 collective-permute-done.2
  54.4 0.6 collective-permute-done.3
  55.2 0.0 all-gather.2.cloned.1.call-done.int_ref
  55.2 8.8 %ladder.3 = bf16[4,4,2,4,32,256]{5,4,3,2,1,0:T(8,128)(2,1)S(1)} custom-call(bf16[4,2,4,32,1024]{4,3,2,1,0:T(8,128)(2,1)S(1)} %bitcast.50, bf16[4,2,32,1024]{3,2,1,0:T(8,128)(2,1)S(1)} %constant_dynamic-slice_fusion.mask_ref, bf16[128,128]{1,0:T(8,128)(2,1)S(1)} %copy-done.1, bf16[2048,2048]{1,0:T(8,128)(2,1)} %all-gather.2.cloned.1.call-done.int_ref), custom_call_target="tpu_custom_call" | custom-call | flops 4563402752 | bytes 12582912 | tf_op jit(solution)/shard_map/ladder/pallas_call | solution.py:60
  64.0 0.0 copy-start
  64.0 1.3 copy-done
  65.3 0.0 reduce-scatter.4.cloned.1.call-update
  65.4 0.2 reduce-scatter.8.cloned.1.call-start
  65.6 5.7 %copy.27 = bf16[32,8,6,1024]{3,0,2,1:T(8,128)(2,1)} copy(bf16[32,8,6,1024]{3,2,1,0:T(8,128)(2,1)} %get-tuple-element.13) | data formatting | bytes 6291456
  71.2 21.0 %all-to-all-done.2 = bf16[8,6,32,1024]{3,2,1,0:T(8,128)(2,1)} async-done(((bf16[8,6,32,1024]{3,2,1,0:T(8,128)(2,1)}), bf16[8,6,32,1024]{3,2,1,0:T(8,128)(2,1)}, u32[]{:S(2)}, u32[]{:S(2)}) %all-to-all-start.2) | async-done | bytes 3145760 | tf_op jit(solution)/shard_map/all_to_all | solution.py:129
  92.2 42.3 %all_to_all.30 = bf16[8,6,32,1024]{3,2,1,0:T(8,128)(2,1)} all-to-all(bf16[8,6,32,1024]{3,2,1,0:T(8,128)(2,1)} %bitcast.55), channel_id=1, replica_groups=mesh['bulk'=4,'z'=4,'core'=2] {'bulk','core'}, dimensions={0} | all-to-all | bytes 6291456 | tf_op jit(solution)/shard_map/all_to_all | solution.py:129
  134.5 12.6 %ladder.5 = bf16[4,4,2,6,32,256]{5,4,3,2,1,0:T(8,128)(2,1)} custom-call(bf16[4,2,6,32,1024]{4,3,2,1,0:T(8,128)(2,1)} %bitcast.59, bf16[4,2,32,1024]{3,2,1,0:T(8,128)(2,1)S(1)} %constant_dynamic-slice_fusion.mask_ref, bf16[128,128]{1,0:T(8,128)(2,1)S(1)} %copy-done.1, bf16[2048,2048]{1,0:T(8,128)(2,1)} %all-gather.2.cloned.1.call-done.int_ref), custom_call_target="tpu_custom_call" | custom-call | flops 6845104128 | bytes 14680064 | tf_op jit(solution)/shard_map/ladder/pallas_call | solution.py:60
  147.1 0.0 reduce-scatter.8.cloned.1.call-update
  147.1 0.0 reduce-scatter.6.cloned.1.call-start
  147.1 12.5 %ladder.4 = bf16[4,4,2,6,32,256]{5,4,3,2,1,0:T(8,128)(2,1)} custom-call(bf16[4,2,6,32,1024]{4,3,2,1,0:T(8,128)(2,1)} %bitcast.12.amp_ref, bf16[4,2,32,1024]{3,2,1,0:T(8,128)(2,1)S(1)} %constant_dynamic-slice_fusion.mask_ref, bf16[128,128]{1,0:T(8,128)(2,1)S(1)} %copy-done.1, bf16[2048,2048]{1,0:T(8,128)(2,1)} %all-gather.2.cloned.1.call-done.int_ref), custom_call_target="tpu_custom_call" | custom-call | flops 6845104128 | bytes 14680064 | tf_op jit(solution)/shard_map/ladder/pallas_call | solution.py:60
  159.7 0.0 reduce-scatter.6.cloned.1.call-update
  159.7 0.0 reduce-scatter.4.cloned.1.call-done
  159.7 13.2 %all_to_all.31 = bf16[8,4,32,256]{3,2,1,0:T(8,128)(2,1)S(1)} all-to-all(bf16[8,4,32,256]{3,2,1,0:T(8,128)(2,1)} %bitcast.64), channel_id=1, replica_groups=mesh['bulk'=4,'z'=4,'core'=2] {'bulk','core'}, dimensions={0} | all-to-all | bytes 1048576 | tf_op jit(solution)/shard_map/all_to_all | solution.py:134
  172.9 34.0 %reduce-scatter.8.cloned.1.call-done = bf16[1,4,2,6,32,256]{5,4,3,2,1,0:T(8,128)(2,1)} async-done(((bf16[4,4,2,6,32,256]{5,4,3,2,1,0:T(8,128)(2,1)}), bf16[1,4,2,6,32,256]{5,4,3,2,1,0:T(8,128)(2,1)}) %reduce-scatter.8.cloned.1.call-update) | async-done | bytes 786448 | tf_op jit(solution)/shard_map/reduce_scatter | solution.py:132
  206.9 3.7 %all-to-all-start.5 = ((bf16[8,6,32,256]{3,2,1,0:T(8,128)(2,1)}), bf16[8,6,32,256]{3,2,1,0:T(8,128)(2,1)S(1)}, u32[]{:S(2)}, u32[]{:S(2)}) async-start(bf16[8,6,32,256]{3,2,1,0:T(8,128)(2,1)} %bitcast.60), calls=%async_computation.8 | async-start | bytes 1572864 | tf_op jit(solution)/shard_map/all_to_all | solution.py:134
  210.5 58.9 %reduce-scatter.6.cloned.1.call-done = bf16[1,4,2,6,32,256]{5,4,3,2,1,0:T(8,128)(2,1)} async-done(((bf16[4,4,2,6,32,256]{5,4,3,2,1,0:T(8,128)(2,1)}), bf16[1,4,2,6,32,256]{5,4,3,2,1,0:T(8,128)(2,1)}) %reduce-scatter.6.cloned.1.call-update) | async-done | bytes 786448 | tf_op jit(solution)/shard_map/reduce_scatter | solution.py:132
  269.5 0.0 all-to-all-done.5
  269.5 16.2 %all_to_all.32 = bf16[8,6,32,256]{3,2,1,0:T(8,128)(2,1)S(1)} all-to-all(bf16[8,6,32,256]{3,2,1,0:T(8,128)(2,1)} %bitcast.61), channel_id=1, replica_groups=mesh['bulk'=4,'z'=4,'core'=2] {'bulk','core'}, dimensions={0} | all-to-all | bytes 1572864 | tf_op jit(solution)/shard_map/all_to_all | solution.py:134
  285.7 0.2 pad_maximum_fusion
  285.9 4.0 %copy.10 = bf16[128,32,256]{0,1,2:T(8,128)(2,1)} copy(bf16[128,32,256]{2,1,0:T(8,128)(2,1)S(1)} %bitcast.57) | data formatting | bytes 4194304 | tf_op jit(solution)/shard_map/reshape | solution.py:136
  289.9 3.9 %copy.29 = bf16[32,8,32,128]{3,1,2,0:T(8,128)(2,1)} copy(bf16[32,8,32,128]{3,2,1,0:T(8,128)(2,1)} %bitcast.58) | data formatting | bytes 4194304
  (18 shorter events, 0.2 us)
Async XLA Ops:
  6.5 48.6 %all-gather.2.cloned.1.call-start = ((), (), s32[]{:S(2)}) async-start(), calls=%async_computation.9 | async-start | bytes 12582912 | tf_op jit(solution)/shard_map/all_gather | solution.py:123
  6.5 2.2 copy-start.2
  17.4 5.3 %copy-start.3 = (s32[32,8]{0,1:T(8,128)S(1)}, s32[32,8]{0,1:T(8,128)}, u32[]{:S(2)}) copy-start(s32[32,8]{0,1:T(8,128)} %param.6) | copy-start | bytes 3076
  17.4 32.5 %all-to-all-start = ((bf16[8,4,32,1024]{3,2,1,0:T(8,128)(2,1)}), bf16[8,4,32,1024]{3,2,1,0:T(8,128)(2,1)S(1)}, u32[]{:S(2)}, u32[]{:S(2)}) async-start(bf16[8,4,32,1024]{3,2,1,0:T(8,128)(2,1)} %bitcast.56), calls=%async_computation | async-start | bytes 4194304 | tf_op jit(solution)/shard_map/all_to_all | solution.py:122
  22.9 1.5 collective-permute-start
  24.4 29.9 %collective-permute-start.1 = (bf16[2,32,1024]{2,1,0:T(8,128)(2,1)S(1)}, bf16[2,32,1024]{2,1,0:T(8,128)(2,1)S(1)}, u32[]{:S(2)}, u32[]{:S(2)}) collective-permute-start(bf16[2,32,1024]{2,1,0:T(8,128)(2,1)S(1)} %pad_maximum_fusion.1), channel_id=1, source_target_pairs={{0,24},{8,0},{16,8},{24,16},{1,25},{9,1},{17,9},{25,17},{2,26},{10... | collective-permute-start | bytes 393224 | tf_op jit(solution)/shard_map/ppermute | solution.py:95
  42.7 11.7 %collective-permute-start.2 = (bf16[2,32,1024]{2,1,0:T(8,128)(2,1)S(1)}, bf16[2,32,1024]{2,1,0:T(8,128)(2,1)S(1)}, u32[]{:S(2)}, u32[]{:S(2)}) collective-permute-start(bf16[2,32,1024]{2,1,0:T(8,128)(2,1)S(1)} %pad_maximum_fusion.1), channel_id=1, source_target_pairs={{0,16},{8,24},{16,0},{24,8},{1,17},{9,25},{17,1},{25,9},{2,18},{10... | collective-permute-start | bytes 393224 | tf_op jit(solution)/shard_map/ppermute | solution.py:95
  43.6 11.4 %collective-permute-start.3 = (bf16[2,32,1024]{2,1,0:T(8,128)(2,1)S(1)}, bf16[2,32,1024]{2,1,0:T(8,128)(2,1)S(1)}, u32[]{:S(2)}, u32[]{:S(2)}) collective-permute-start(bf16[2,32,1024]{2,1,0:T(8,128)(2,1)S(1)} %pad_maximum_fusion.1), channel_id=1, source_target_pairs={{0,8},{8,16},{16,24},{24,0},{1,9},{9,17},{17,25},{25,1},{2,10},{10... | collective-permute-start | bytes 393224 | tf_op jit(solution)/shard_map/ppermute | solution.py:95
  49.9 42.3 %all-to-all-start.2 = ((bf16[8,6,32,1024]{3,2,1,0:T(8,128)(2,1)}), bf16[8,6,32,1024]{3,2,1,0:T(8,128)(2,1)}, u32[]{:S(2)}, u32[]{:S(2)}) async-start(bf16[8,6,32,1024]{3,2,1,0:T(8,128)(2,1)} %bitcast.54), calls=%async_computation.3 | async-start | bytes 6291456 | tf_op jit(solution)/shard_map/all_to_all | solution.py:129
  54.3 0.9 copy-start.1
  54.3 105.4 %reduce-scatter.4.cloned.1.call-start = ((), (), s32[]{:S(2)}) async-start(), calls=%async_computation.10 | async-start | bytes 2621440 | tf_op jit(solution)/shard_map/reduce_scatter | solution.py:132
  64.0 1.3 copy-start
  65.4 141.5 %reduce-scatter.8.cloned.1.call-start = ((), (), s32[]{:S(2)}) async-start(), calls=%async_computation.12 | async-start | bytes 3932160 | tf_op jit(solution)/shard_map/reduce_scatter | solution.py:132
  147.1 122.4 %reduce-scatter.6.cloned.1.call-start = ((), (), s32[]{:S(2)}) async-start(), calls=%async_computation.11 | async-start | bytes 3932160 | tf_op jit(solution)/shard_map/reduce_scatter | solution.py:132
  206.9 62.6 %all-to-all-start.5 = ((bf16[8,6,32,256]{3,2,1,0:T(8,128)(2,1)}), bf16[8,6,32,256]{3,2,1,0:T(8,128)(2,1)S(1)}, u32[]{:S(2)}, u32[]{:S(2)}) async-start(bf16[8,6,32,256]{3,2,1,0:T(8,128)(2,1)} %bitcast.60), calls=%async_computation.8 | async-start | bytes 1572864 | tf_op jit(solution)/shard_map/all_to_all | solution.py:134
Sparse Core Ops, SparseCore 0:
  11.7 22.5 all-gather.1
  65.5 45.3 reduce-scatter.3
  147.2 59.6 reduce-scatter.7
  209.1 60.2 reduce-scatter.5

commit v5 on v4

--- a/solution.py
+++ b/solution.py
@@ -124,11 +124,15 @@
     mask = gather_maps(jnp.repeat(amp_tiles.astype(jnp.bfloat16), TILE, axis=1), peers, cores)
     finished = []
     for at, step in enumerate(sizes):
-        if at + 1 < len(sizes):
-            arrived, ready = lax.optimization_barrier((arrived, sent[at + 1]))
-            following = swap(ready)
+        ahead = at + 1 < len(sizes)
+        if at == 0 and ahead:
+            arrived, *sent[1:] = lax.optimization_barrier((arrived, *sent[1:]))
+            following = swap(sent[1])
         arrived = arrived.reshape(peers, cores, step, first_dev, local_cols)
         partial = ladder(arrived, mask, occ_coupling, int_kept, owners)
+        if at > 0 and ahead:
+            partial, ready = lax.optimization_barrier((partial, sent[at + 1]))
+            following = swap(ready)
         total = lax.psum_scatter(partial, "z", scatter_dimension=0, tiled=False)
         width = total.shape[-1]
         finished.append(swap(total.reshape(group, step, first_dev, width)))

time: 301 us -> 275 us (0.914)
  waiting for transfers between devices: 120 us -> 45.7 us
  blocking collectives: 71.7 us -> 130 us
  starting transfers between devices: 19.6 us -> 9.61 us
    reduce_scatter x3, waiting for transfers between devices: 92.9 us -> 38.3 us  [shards(): total = lax.psum_scatter(partial, 'z', scatter_dimension=0, tiled=False)]
    all_to_all x0 -> x1, blocking collectives: none -> 42.3 us  [shards(): following = swap(sent[1])]
    all_to_all x2 -> x0, waiting for transfers between devices: 21 us -> none  [the longest x1 21 us: shards(): following = swap(ready)]
    all_to_all x2 -> x3, blocking collectives: 29.4 us -> 45.4 us  [shards(): finished.append(swap(total.reshape(group, step, first_dev, width)))]
    unnamed x19 -> x17, local copies, waits for them, and re-layouts: 19.9 us -> 9.17 us
    transpose x0 -> x1, local copies, waits for them, and re-layouts: none -> 10.3 us  [shards(): sent.append(by_owner[:, :, begin:begin + step].transpose(1, 2, 0, 3))]
    all_to_all x2 -> x0, starting transfers between devices: 8.1 us -> none  [the longest x1 4.45 us: shards(): following = swap(ready)]
    ppermute x3, waiting for transfers between devices: 0.57 us -> 7.27 us  [gather_maps(): lax.ppermute(pair, 'bulk', [(at, (at + shift) % peers) for at in range(pe...]
  transfers between devices with their start and end apart: 11 -> 9, of which waited for: 6 -> 3; matrix products, arithmetic and copies ran while one was open for 9% -> 10% of each run, Pallas kernels for 11% -> 9%
where the time goes in v5:
time: 275 us
  blocking collectives  130 us (47%)
  waiting for transfers between devices  45.7 us (17%)
  local copies, waits for them, and re-layouts  38.2 us (14%)
  Pallas kernels  34 us (12%)
  between operations  13.3 us (5%)
  starting transfers between devices  9.61 us (3%)
  other arithmetic  4.01 us (1%)
    all_to_all x3, blocking collectives, shards(): finished.append(swap(total.reshape(group, step, first_dev, width)))  45.4 us
    all_to_all x1, blocking collectives, shards(): following = swap(sent[1])  42.3 us
    all_to_all x1, blocking collectives, shards(): following = swap(ready)  42.3 us
    reduce_scatter x3, waiting for transfers between devices, shards(): total = lax.psum_scatter(partial, 'z', scatter_dimension=0, tiled=False)  38.3 us
    pallas_call x3, Pallas kernels, ladder(): pl.pallas_call(functools.partial(ladder_kernel, rows_at), grid=(seconds /...  34 us
    slice x2, local copies, waits for them, and re-layouts, shards(): sent.append(by_owner[:, :, begin:begin + step].transpose(1, 2, 0, 3))  13.9 us
    transpose x1, local copies, waits for them, and re-layouts, shards(): sent.append(by_owner[:, :, begin:begin + step].transpose(1, 2, 0, 3))  10.3 us
    unnamed x17, local copies, waits for them, and re-layouts  9.17 us
  transfers between devices with their start and end apart: 9, of which 3 were waited for; matrix products, arithmetic and copies ran while one was open for 10% of the time, Pallas kernels for 9%

profile of v5, /device:TPU:0, one launch (start us, length us, event | category | flops | bytes accessed | tf_op | source)
XLA Modules:
  0.0 274.7 jit_solution(16727607732093919313)
XLA Ops:
  6.5 0.0 all-gather.2.cloned.1.call-start
  6.5 0.0 copy-start.2
  6.5 0.8 convert_element_type.7
  7.4 0.6 mul.11
  8.0 0.7 copy-done.2
  8.7 2.9 %bitcast_multiply_fusion = bf16[1024,2048]{1,0:T(8,128)(2,1)} fusion(bf16[1024,2048]{1,0:T(8,128)(2,1)S(1)} %copy-done.2, bf16[128,8,16,128]{3,2,1,0:T(8,128)(2,1)S(1)} %bitcast.49), kind=kLoop, calls=%fused_computation | loop fusion | flops 2097152 | bytes 12582912 | tf_op jit(solution)/shard_map/mul | solution.py:18
  11.6 0.0 all-gather.2.cloned.1.call-update
  11.7 0.7 copy-done.3
  12.3 0.1 copy.9
  12.4 0.1 broadcast_in_dim.4
  12.5 0.5 collective-permute-start
  13.1 3.3 %slice.12 = bf16[32,8,4,1024]{3,2,1,0:T(4,128)(2,1)S(1)} slice(bf16[32,8,16,1024]{3,2,1,0:T(8,128)(2,1)} %bitcast.50), slice={[0:32], [0:8], [0:4], [0:1024]} | slice | bytes 4194304 | tf_op jit(solution)/shard_map/slice | solution.py:120
  16.4 2.5 copy.28
  18.8 4.8 %all-to-all-start = ((bf16[8,4,32,1024]{3,2,1,0:T(8,128)(2,1)}), bf16[8,4,32,1024]{3,2,1,0:T(8,128)(2,1)S(1)}, u32[]{:S(2)}, u32[]{:S(2)}) async-start(bf16[8,4,32,1024]{3,2,1,0:T(8,128)(2,1)} %bitcast.52), calls=%async_computation | async-start | bytes 4194304 | tf_op jit(solution)/shard_map/all_to_all | solution.py:122
  23.7 0.0 reduce-scatter.4.cloned.1.call-start
  23.7 10.6 %fusion = (bf16[32,8,6,1024]{3,2,1,0:T(8,128)(2,1)}, bf16[32,8,6,1024]{3,2,1,0:T(8,128)(2,1)}) fusion(bf16[32,8,16,1024]{3,2,1,0:T(8,128)(2,1)} %bitcast.51), kind=kLoop, calls=%fused_computation.19 | loop fusion | bytes 12582912 | tf_op jit(solution)/shard_map/slice | solution.py:120
  34.3 0.0 collective-permute-done
  34.4 3.0 %collective-permute-start.1 = (bf16[2,32,1024]{2,1,0:T(8,128)(2,1)S(1)}, bf16[2,32,1024]{2,1,0:T(8,128)(2,1)S(1)}, u32[]{:S(2)}, u32[]{:S(2)}) collective-permute-start(bf16[2,32,1024]{2,1,0:T(8,128)(2,1)S(1)} %pad_maximum_fusion.1), channel_id=1, source_target_pairs={{0,24},{8,0},{16,8},{24,16},{1,25},{9,1},{17,9},{25,17},{2,26},{10... | collective-permute-start | bytes 393224 | tf_op jit(solution)/shard_map/ppermute | solution.py:95
  37.4 10.3 %copy_bitcast_fusion = (bf16[8,6,32,1024]{3,2,1,0:T(8,128)(2,1)}, bf16[8,6,32,1024]{3,2,1,0:T(8,128)(2,1)}) fusion(bf16[32,8,6,1024]{3,2,1,0:T(8,128)(2,1)} %get-tuple-element.15, bf16[32,8,6,1024]{3,2,1,0:T(8,128)(2,1)} %get-tuple-element.16), kind=kLoop, calls=%fused_computation.1 | loop fusion | bytes 12582912 | tf_op jit(solution)/shard_map/transpose | solution.py:120
  47.6 0.0 copy-start.1
  47.6 0.6 collective-permute-start.2
  48.2 0.6 collective-permute-start.3
  48.8 3.9 %collective-permute-done.1 = bf16[2,32,1024]{2,1,0:T(8,128)(2,1)S(1)} collective-permute-done((bf16[2,32,1024]{2,1,0:T(8,128)(2,1)S(1)}, bf16[2,32,1024]{2,1,0:T(8,128)(2,1)S(1)}, u32[]{:S(2)}, u32[]{:S(2)}) %collective-permute-start.1) | collective-permute-done | bytes 131104 | tf_op jit(solution)/shard_map/ppermute | solution.py:95
  52.7 3.3 %collective-permute-done.2 = bf16[2,32,1024]{2,1,0:T(8,128)(2,1)S(1)} collective-permute-done((bf16[2,32,1024]{2,1,0:T(8,128)(2,1)S(1)}, bf16[2,32,1024]{2,1,0:T(8,128)(2,1)S(1)}, u32[]{:S(2)}, u32[]{:S(2)}) %collective-permute-start.2) | collective-permute-done | bytes 131104 | tf_op jit(solution)/shard_map/ppermute | solution.py:95
  56.1 0.0 collective-permute-done.3
  56.2 0.0 all-to-all-done
  56.3 0.0 all-gather.2.cloned.1.call-done.int_ref
  56.3 0.0 copy-done.1
  56.3 8.8 %ladder.3 = bf16[4,4,2,4,32,256]{5,4,3,2,1,0:T(8,128)(2,1)S(1)} custom-call(bf16[4,2,4,32,1024]{4,3,2,1,0:T(8,128)(2,1)S(1)} %bitcast.48, bf16[4,2,32,1024]{3,2,1,0:T(8,128)(2,1)S(1)} %constant_dynamic-slice_fusion.mask_ref, bf16[128,128]{1,0:T(8,128)(2,1)S(1)} %copy-done.1, bf16[2048,2048]{1,0:T(8,128)(2,1)} %all-gather.2.cloned.1.call-done.int_ref), custom_call_target="tpu_custom_call" | custom-call | flops 4563402752 | bytes 12582912 | tf_op jit(solution)/shard_map/ladder/pallas_call | solution.py:60
  65.1 0.0 copy-start
  65.1 1.3 copy-done
  66.4 0.0 reduce-scatter.4.cloned.1.call-update
  66.5 0.0 reduce-scatter.6.cloned.1.call-start
  66.5 42.3 %all_to_all.30 = bf16[8,6,32,1024]{3,2,1,0:T(8,128)(2,1)} all-to-all(bf16[8,6,32,1024]{3,2,1,0:T(8,128)(2,1)} %get-tuple-element.11), channel_id=1, replica_groups=mesh['bulk'=4,'z'=4,'core'=2] {'bulk','core'}, dimensions={0} | all-to-all | bytes 6291456 | tf_op jit(solution)/shard_map/all_to_all | solution.py:130
  108.8 12.6 %ladder.4 = bf16[4,4,2,6,32,256]{5,4,3,2,1,0:T(8,128)(2,1)} custom-call(bf16[4,2,6,32,1024]{4,3,2,1,0:T(8,128)(2,1)} %bitcast.56, bf16[4,2,32,1024]{3,2,1,0:T(8,128)(2,1)S(1)} %constant_dynamic-slice_fusion.mask_ref, bf16[128,128]{1,0:T(8,128)(2,1)S(1)} %copy-done.1, bf16[2048,2048]{1,0:T(8,128)(2,1)} %all-gather.2.cloned.1.call-done.int_ref), custom_call_target="tpu_custom_call" | custom-call | flops 6845104128 | bytes 14680064 | tf_op jit(solution)/shard_map/ladder/pallas_call | solution.py:60
  121.4 0.0 reduce-scatter.6.cloned.1.call-update
  121.4 0.0 reduce-scatter.8.cloned.1.call-start
  121.4 42.3 %all_to_all.31 = bf16[8,6,32,1024]{3,2,1,0:T(8,128)(2,1)} all-to-all(bf16[8,6,32,1024]{3,2,1,0:T(8,128)(2,1)} %get-tuple-element.14), channel_id=1, replica_groups=mesh['bulk'=4,'z'=4,'core'=2] {'bulk','core'}, dimensions={0} | all-to-all | bytes 6291456 | tf_op jit(solution)/shard_map/all_to_all | solution.py:135
  163.7 12.6 %ladder.5 = bf16[4,4,2,6,32,256]{5,4,3,2,1,0:T(8,128)(2,1)} custom-call(bf16[4,2,6,32,1024]{4,3,2,1,0:T(8,128)(2,1)} %bitcast.55, bf16[4,2,32,1024]{3,2,1,0:T(8,128)(2,1)S(1)} %constant_dynamic-slice_fusion.mask_ref, bf16[128,128]{1,0:T(8,128)(2,1)S(1)} %copy-done.1, bf16[2048,2048]{1,0:T(8,128)(2,1)} %all-gather.2.cloned.1.call-done.int_ref), custom_call_target="tpu_custom_call" | custom-call | flops 6845104128 | bytes 14680064 | tf_op jit(solution)/shard_map/ladder/pallas_call | solution.py:60
  176.3 0.0 reduce-scatter.8.cloned.1.call-update
  176.3 0.0 reduce-scatter.4.cloned.1.call-done
  176.4 13.2 %all_to_all.32 = bf16[8,4,32,256]{3,2,1,0:T(8,128)(2,1)S(1)} all-to-all(bf16[8,4,32,256]{3,2,1,0:T(8,128)(2,1)} %bitcast.61), channel_id=1, replica_groups=mesh['bulk'=4,'z'=4,'core'=2] {'bulk','core'}, dimensions={0} | all-to-all | bytes 1048576 | tf_op jit(solution)/shard_map/all_to_all | solution.py:138
  189.5 16.0 %all_to_all.33 = bf16[8,6,32,256]{3,2,1,0:T(8,128)(2,1)S(1)} all-to-all(bf16[8,6,32,256]{3,2,1,0:T(8,128)(2,1)} %bitcast.57), channel_id=1, replica_groups=mesh['bulk'=4,'z'=4,'core'=2] {'bulk','core'}, dimensions={0} | all-to-all | bytes 1572864 | tf_op jit(solution)/shard_map/all_to_all | solution.py:138
  205.5 38.3 %reduce-scatter.8.cloned.1.call-done = bf16[1,4,2,6,32,256]{5,4,3,2,1,0:T(8,128)(2,1)} async-done(((bf16[4,4,2,6,32,256]{5,4,3,2,1,0:T(8,128)(2,1)}), bf16[1,4,2,6,32,256]{5,4,3,2,1,0:T(8,128)(2,1)}) %reduce-scatter.8.cloned.1.call-update) | async-done | bytes 786448 | tf_op jit(solution)/shard_map/reduce_scatter | solution.py:136
  243.8 16.2 %all_to_all.34 = bf16[8,6,32,256]{3,2,1,0:T(8,128)(2,1)S(1)} all-to-all(bf16[8,6,32,256]{3,2,1,0:T(8,128)(2,1)} %bitcast.58), channel_id=1, replica_groups=mesh['bulk'=4,'z'=4,'core'=2] {'bulk','core'}, dimensions={0} | all-to-all | bytes 1572864 | tf_op jit(solution)/shard_map/all_to_all | solution.py:138
  260.0 0.2 pad_maximum_fusion
  260.2 4.0 %copy.10 = bf16[128,32,256]{0,1,2:T(8,128)(2,1)} copy(bf16[128,32,256]{2,1,0:T(8,128)(2,1)S(1)} %bitcast.53) | data formatting | bytes 4194304 | tf_op jit(solution)/shard_map/reshape | solution.py:140
  264.2 3.9 %copy.27 = bf16[32,8,32,128]{3,1,2,0:T(8,128)(2,1)} copy(bf16[32,8,32,128]{3,2,1,0:T(8,128)(2,1)} %bitcast.54) | data formatting | bytes 4194304
  (15 shorter events, 0.2 us)
Async XLA Ops:
  6.5 49.7 %all-gather.2.cloned.1.call-start = ((), (), s32[]{:S(2)}) async-start(), calls=%async_computation.9 | async-start | bytes 12582912 | tf_op jit(solution)/shard_map/all_gather | solution.py:123
  6.5 2.2 copy-start.2
  11.6 0.7 copy-start.3
  12.5 21.8 %collective-permute-start = (bf16[32,1024]{1,0:T(8,128)(2,1)S(1)}, bf16[32,1024]{1,0:T(8,128)(2,1)S(1)}, u32[]{:S(2)}, u32[]{:S(2)}) collective-permute-start(bf16[32,1024]{1,0:T(8,128)(2,1)S(1)} %bitcast.62), channel_id=1, source_target_pairs={{0,1},{1,0},{2,3},{3,2},{4,5},{5,4},{6,7},{7,6},{8,9},{9,8},{10,11... | collective-permute-start | bytes 196616 | tf_op jit(solution)/shard_map/ppermute | solution.py:91
  18.8 37.4 %all-to-all-start = ((bf16[8,4,32,1024]{3,2,1,0:T(8,128)(2,1)}), bf16[8,4,32,1024]{3,2,1,0:T(8,128)(2,1)S(1)}, u32[]{:S(2)}, u32[]{:S(2)}) async-start(bf16[8,4,32,1024]{3,2,1,0:T(8,128)(2,1)} %bitcast.52), calls=%async_computation | async-start | bytes 4194304 | tf_op jit(solution)/shard_map/all_to_all | solution.py:122
  23.7 152.7 %reduce-scatter.4.cloned.1.call-start = ((), (), s32[]{:S(2)}) async-start(), calls=%async_computation.10 | async-start | bytes 2621440 | tf_op jit(solution)/shard_map/reduce_scatter | solution.py:136
  34.4 18.3 %collective-permute-start.1 = (bf16[2,32,1024]{2,1,0:T(8,128)(2,1)S(1)}, bf16[2,32,1024]{2,1,0:T(8,128)(2,1)S(1)}, u32[]{:S(2)}, u32[]{:S(2)}) collective-permute-start(bf16[2,32,1024]{2,1,0:T(8,128)(2,1)S(1)} %pad_maximum_fusion.1), channel_id=1, source_target_pairs={{0,24},{8,0},{16,8},{24,16},{1,25},{9,1},{17,9},{25,17},{2,26},{10... | collective-permute-start | bytes 393224 | tf_op jit(solution)/shard_map/ppermute | solution.py:95
  47.6 8.6 %copy-start.1 = (bf16[128,128]{1,0:T(8,128)(2,1)S(1)}, bf16[128,128]{1,0:T(8,128)(2,1)}, u32[]{:S(2)}) copy-start(bf16[128,128]{1,0:T(8,128)(2,1)} %occ_ref.5) | copy-start | bytes 98308
  47.6 8.4 %collective-permute-start.2 = (bf16[2,32,1024]{2,1,0:T(8,128)(2,1)S(1)}, bf16[2,32,1024]{2,1,0:T(8,128)(2,1)S(1)}, u32[]{:S(2)}, u32[]{:S(2)}) collective-permute-start(bf16[2,32,1024]{2,1,0:T(8,128)(2,1)S(1)} %pad_maximum_fusion.1), channel_id=1, source_target_pairs={{0,16},{8,24},{16,0},{24,8},{1,17},{9,25},{17,1},{25,9},{2,18},{10... | collective-permute-start | bytes 393224 | tf_op jit(solution)/shard_map/ppermute | solution.py:95
  48.2 7.9 %collective-permute-start.3 = (bf16[2,32,1024]{2,1,0:T(8,128)(2,1)S(1)}, bf16[2,32,1024]{2,1,0:T(8,128)(2,1)S(1)}, u32[]{:S(2)}, u32[]{:S(2)}) collective-permute-start(bf16[2,32,1024]{2,1,0:T(8,128)(2,1)S(1)} %pad_maximum_fusion.1), channel_id=1, source_target_pairs={{0,8},{8,16},{16,24},{24,0},{1,9},{9,17},{17,25},{25,1},{2,10},{10... | collective-permute-start | bytes 393224 | tf_op jit(solution)/shard_map/ppermute | solution.py:95
  65.1 1.3 copy-start
  66.5 123.1 %reduce-scatter.6.cloned.1.call-start = ((), (), s32[]{:S(2)}) async-start(), calls=%async_computation.11 | async-start | bytes 3932160 | tf_op jit(solution)/shard_map/reduce_scatter | solution.py:136
  121.4 122.4 %reduce-scatter.8.cloned.1.call-start = ((), (), s32[]{:S(2)}) async-start(), calls=%async_computation.12 | async-start | bytes 3932160 | tf_op jit(solution)/shard_map/reduce_scatter | solution.py:136
Sparse Core Ops, SparseCore 0:
  11.8 22.5 all-gather.1
  66.6 43.3 reduce-scatter.3
  121.5 59.6 reduce-scatter.5
  183.5 60.2 reduce-scatter.7
